TPU v7x, 128 devices: a whole 4x4x4 slice. The times are simulated.
128 devices in a mesh: slide: 4 (over z_hi, core), space: 32 (over y, x, z_lo).
Axes of the slice: x: 4, y: 4, z: 4 (z_hi: 2, z_lo: 2; z = z_hi * 2 + z_lo), core: 2. Of those that a mesh axis runs over, the one named last changes fastest.
Arguments:
- features: bfloat16 [4, 32, 8, 256, 192], P('slide', 'space'), may hold values from -16 to 16
- dw_kernel: float32 [7, 7, 192], replicated, may hold values from -1.3 to 1.3
- dw_bias: float32 [192], replicated, may hold values from -4 to 4
- ln_gain: float32 [192], replicated, may hold values from 0.5 to 1.5
- ln_bias: float32 [192], replicated, may hold values from -3 to 3
- w_in: bfloat16 [192, 768], replicated, may hold values from -0.4375 to 0.4375
- b_in: float32 [768], replicated, may hold values from -3 to 3
- w_out: bfloat16 [768, 192], replicated, may hold values from -0.21875 to 0.21875
- b_out: float32 [192], replicated, may hold values from -3 to 3
- layer_scale: float32 [192], replicated, may hold values from 0.5 to 1.5
- cotangent: bfloat16 [4, 32, 8, 256, 192], P('slide', 'space'), may hold values from -6 to 6
Outputs:
- block_output: bfloat16 [4, 32, 8, 256, 192], P('slide', 'space')
- grad_input: bfloat16 [4, 32, 8, 256, 192], P('slide', 'space')
- grad_w_in: float32 [192, 768], replicated
- grad_w_out: float32 [768, 192], replicated
- grad_kernel: float32 [7, 7, 192], replicated
All inputs are finite; a program needn't handle non-finite values.
Results may differ from a plain program's by a relative error of at most 0.0068.
Values may be sent and summed in bfloat16 or wider, within the bound.
A program may use at most 64 MiB of HBM per device.

v0:
```python
import jax
import jax.numpy as jnp
from jax import lax
from jax.experimental import pallas as pl
from jax.experimental.pallas import tpu as pltpu
from jax.sharding import PartitionSpec as P

EPSILON = 1e-06
F32 = jnp.float32
BF16 = jnp.bfloat16
MESH = pl.DeviceIdType.MESH
PIXEL_SCALE = float(262144) ** (-0.5)
TILES = 160
NT = (((1,), (1,)), ((), ()))


def remote(src, dst, send, recv, slide, space):
    return pltpu.make_async_remote_copy(
        src_ref=src, dst_ref=dst, send_sem=send, recv_sem=recv,
        device_id={"slide": slide, "space": space}, device_id_type=MESH,
    )


def gelu_parts(h):
    cdf = 0.5 * (1.0 + lax.erf(h * 0.7071067811865476))
    slope = cdf + h * jnp.exp(-0.5 * h * h) * 0.3989422804014327
    return h * cdf, slope


def lay_out(row, wide, packed, value):
    wide[row, 8:264, :] = value[:, :128]
    tail = value[:, 128:192]
    none = jnp.zeros((8, 64), F32)
    packed[row, 8:136, :] = jnp.concatenate([tail[:128], tail[128:]], axis=1)
    packed[row, 0:8, :] = jnp.concatenate([none, tail[120:128]], axis=1)
    packed[row, 136:144, :] = jnp.concatenate([tail[128:136], none], axis=1)


def conv_block(src, taps, start, flip):
    sums = [jnp.zeros((16, 128), F32) for _ in range(8)]
    for b in range(7):
        held = [taps[(6 - a) * 7 + (6 - b) if flip else a * 7 + b] for a in range(7)]
        held = [jnp.concatenate([k, k], axis=0) for k in held]
        for r in range(14):
            v = src[r, pl.ds(start + 5 + b, 16), :]
            for a in range(7):
                if 0 <= r - a < 8:
                    sums[r - a] = sums[r - a] + v * held[a]
    return sums


def kernel(
    feat, cot, dwk, dwb, gain, lbias, w_in, b_in, w_out, b_out, lscale,
    out_block, out_gin, out_gwi, out_gwoT, out_gk,
    fx, ct, xa, xb, ka, kb, za, zc, gza, gzb, par, win, wout, gout, goutT,
    nb, unit, inv, hid, gact, act, gh, outs, gzs, gwi, gwoT, gka, gkb, gia, gib,
    pay, r0, s1, r1, s2, r2, s3, r3, full, halo,
    in_sem, out_sem, halo_send, halo_recv, core_sem, x_send, x_recv, y_send, y_recv, z_send, z_recv,
):
    s, t = lax.axis_index("slide"), lax.axis_index("space")
    z_hi, core = s // 2, s % 2
    z_lo, x, y = t % 2, (t // 2) % 4, t // 8
    z = z_hi * 2 + z_lo
    partner = z_hi * 2 + (1 - core)
    x_peers = [(s, (y * 4 + (x + d) % 4) * 2 + z_lo) for d in (1, 2, 3)]
    y_peers = [(s, (((y + d) % 4) * 4 + x) * 2 + z_lo) for d in (1, 2, 3)]
    z_peers = [(((z + d) % 4) // 2 * 2 + core, (y * 4 + x) * 2 + ((z + d) % 4) % 2) for d in (1, 2, 3)]
    has_up, has_down = t > 0, t < 31
    up, down = jnp.maximum(t - 1, 0), jnp.minimum(t + 1, 31)

    barrier = pltpu.get_barrier_semaphore()
    for ps, pt in [(partner, t)] + x_peers + y_peers + z_peers:
        pl.semaphore_signal(barrier, inc=1, device_id={"slide": ps, "space": pt}, device_id_type=MESH)

    @pl.when(has_up)
    def _():
        pl.semaphore_signal(barrier, inc=1, device_id={"slide": s, "space": up}, device_id_type=MESH)

    @pl.when(has_down)
    def _():
        pl.semaphore_signal(barrier, inc=1, device_id={"slide": s, "space": down}, device_id_type=MESH)

    own_in = pltpu.make_async_copy(feat.at[0, 0], fx.at[pl.ds(3, 8)], in_sem.at[0])
    own_in.start()
    cot_in = pltpu.make_async_copy(cot.at[0, 0], ct, in_sem.at[1])
    cot_in.start()

    pl.semaphore_wait(barrier, 10 + jnp.minimum(t, 1) + jnp.minimum(31 - t, 1))

    to_up = remote(feat.at[0, 0, pl.ds(0, 3)], fx.at[pl.ds(11, 3)], halo_send.at[0], halo_recv.at[0], s, up)
    to_down = remote(feat.at[0, 0, pl.ds(5, 3)], fx.at[pl.ds(0, 3)], halo_send.at[1], halo_recv.at[1], s, down)

    @pl.when(has_up)
    def _():
        to_up.start()

    @pl.when(has_down)
    def _():
        to_down.start()

    par[...] = jnp.zeros_like(par)
    for n, ref in enumerate((dwb, gain, lbias, b_out, lscale)):
        par[n : n + 1, 0:192] = ref[...]
    win[0:192, :] = w_in[...]
    win[192:256, :] = jnp.zeros((64, 768), BF16)
    wout[:, 0:192] = w_out[...]
    wout[:, 192:256] = jnp.zeros((768, 64), BF16)
    for a in range(7):
        for b in range(7):
            k = dwk[a, b : b + 1, :]
            ka[a * 7 + b] = jnp.broadcast_to(k[:, 0:128], (8, 128))
            tail = k[:, 128:192]
            kb[a * 7 + b] = jnp.broadcast_to(jnp.concatenate([tail, tail], axis=1), (8, 128))

    def clear(r, _):
        zeros = jnp.zeros((8, 128), F32)
        for ref in (xa, gza):
            ref[r, 0:8, :] = zeros
            ref[r, 264:272, :] = zeros
        return 0

    lax.fori_loop(0, 14, clear, 0)
    gwi[...] = jnp.zeros_like(gwi)
    gwoT[...] = jnp.zeros_like(gwoT)
    gka[...] = jnp.zeros_like(gka)
    gkb[...] = jnp.zeros_like(gkb)

    cot_in.wait()

    def scale_row(i, _):
        g = (par[4:5, 0:192] * ct[i].astype(F32)).astype(BF16)
        gout[i, :, 0:192] = g
        gout[i, :, 192:256] = jnp.zeros((256, 64), BF16)
        goutT[i] = g.T
        return 0

    lax.fori_loop(0, 8, scale_row, 0)
    own_in.wait()

    @pl.when(has_up)
    def _():
        to_down.wait_recv()

    @pl.when(t == 0)
    def _():
        fx[0:3] = jnp.zeros((3, 256, 192), BF16)

    @pl.when(has_down)
    def _():
        to_up.wait_recv()

    @pl.when(t == 31)
    def _():
        fx[11:14] = jnp.zeros((3, 256, 192), BF16)

    def lay_row(r, _):
        lay_out(r, xa, xb, fx[r].astype(F32))
        return 0

    lax.fori_loop(0, 14, lay_row, 0)

    def conv_a(n, _):
        start = pl.multiple_of(n * 16, 16)
        sums = conv_block(xa, ka, start, False)
        for i in range(8):
            za[i, pl.ds(start, 16), :] = sums[i] + par[0:1, 0:128]
        return 0

    lax.fori_loop(0, 16, conv_a, 0)

    def conv_b(n, _):
        start = pl.multiple_of(n * 16, 16)
        sums = conv_block(xb, kb, start, False)
        lower = lax.broadcasted_iota(jnp.int32, (16, 128), 1) < 64
        for i in range(8):
            zc[i, pl.ds(start, 16), :] = jnp.where(lower, sums[i] + par[0:1, 128:256], 0.0)
            zc[i, pl.ds(start + 128, 16), :] = jnp.where(lower, pltpu.roll(sums[i], 64, 1) + par[0:1, 128:256], 0.0)
        return 0

    lax.fori_loop(0, 8, conv_b, 0)

    def mlp_row(i, _):
        def norm(q, _):
            px = pl.ds(pl.multiple_of(q * 64, 64), 64)
            a, c = za[i, px, :], zc[i, px, :]
            lower = lax.broadcasted_iota(jnp.int32, (64, 128), 1) < 64
            mean = jnp.sum(a + c, axis=1, keepdims=True) * (1.0 / 192)
            a = a - mean
            c = jnp.where(lower, c - mean, 0.0)
            var = jnp.sum(a * a + c * c, axis=1, keepdims=True) * (1.0 / 192)
            r = lax.rsqrt(var + EPSILON)
            a, c = a * r, c * r
            unit[px, 0:128] = a
            unit[px, 128:256] = c
            inv[px, :] = jnp.broadcast_to(r, (64, 128))
            nb[px, 0:128] = (a * par[1:2, 0:128] + par[2:3, 0:128]).astype(BF16)
            nb[px, 128:256] = (c * par[1:2, 128:256] + par[2:3, 128:256]).astype(BF16)
            return 0

        lax.fori_loop(0, 4, norm, 0)
        hid[...] = jnp.dot(nb[...], win[...], preferred_element_type=F32)
        gact[...] = lax.dot_general(gout[i], wout[...], NT, preferred_element_type=F32)

        def gelu(n, _):
            px = pl.ds(pl.multiple_of((n // 2) * 16, 16), 16)
            ln = pl.ds(pl.multiple_of((n % 2) * 384, 384), 384)
            h = hid[px, ln] + b_in[0:1, ln]
            value, slope = gelu_parts(h)
            act[px, ln] = value.astype(BF16)
            gh[px, ln] = (gact[px, ln] * slope).astype(BF16)
            return 0

        lax.fori_loop(0, 32, gelu, 0)
        hid[:, 0:256] = jnp.dot(act[...], wout[...], preferred_element_type=F32)
        hid[:, 256:512] = lax.dot_general(gh[...], win[...], NT, preferred_element_type=F32)
        gwi[...] += jnp.dot(nb[:, 0:192].T, gh[...], preferred_element_type=F32)
        gwoT[...] += jnp.dot(goutT[i], act[...], preferred_element_type=F32)

        def finish(q, _):
            px = pl.ds(pl.multiple_of(q * 64, 64), 64)
            branch = (hid[px, 0:256] + par[3:4, :])[:, 0:192]
            outs[i, px, :] = (fx[i + 3, px, :].astype(F32) + par[4:5, 0:192] * branch).astype(BF16)
            gn = hid[px, 256:512] * par[1:2, :]
            u = unit[px, :]
            m1 = jnp.sum(gn[:, :128] + gn[:, 128:], axis=1, keepdims=True) * (1.0 / 192)
            gu = gn * u
            m2 = jnp.sum(gu[:, :128] + gu[:, 128:], axis=1, keepdims=True) * (1.0 / 192)
            r = inv[px, :]
            gz = (gn - m1 - u * m2) * jnp.concatenate([r, r], axis=1)
            gzs[i, px, :] = gz[:, 0:192].astype(BF16)
            return 0

        lax.fori_loop(0, 4, finish, 0)
        lay_out(i + 3, gza, gzb, gzs[i].astype(F32))
        return 0

    lax.fori_loop(0, 8, mlp_row, 0)
    block_out = pltpu.make_async_copy(outs, out_block.at[0, 0], out_sem.at[0])
    block_out.start()

    gz_up = remote(gzs.at[pl.ds(0, 3)], halo.at[1], halo_send.at[2], halo_recv.at[2], s, up)
    gz_down = remote(gzs.at[pl.ds(5, 3)], halo.at[0], halo_send.at[3], halo_recv.at[3], s, down)

    @pl.when(has_up)
    def _():
        gz_up.start()

    @pl.when(has_down)
    def _():
        gz_down.start()

    def taps_grad(src, grad, total):
        def step(n, _):
            start = pl.multiple_of(n * 16, 16)
            g = [grad[i + 3, pl.ds(start + 8, 16), :] for i in range(8)]
            for b in range(7):
                sums = [None] * 7
                for r in range(14):
                    v = src[r, pl.ds(start + 5 + b, 16), :]
                    for a in range(7):
                        if 0 <= r - a < 8:
                            p = g[r - a] * v
                            sums[a] = p if sums[a] is None else sums[a] + p
                for a in range(7):
                    total[a * 7 + b] += sums[a][0:8] + sums[a][8:16]
            return 0

        return step

    lax.fori_loop(0, 16, taps_grad(xa, gza, gka), 0)
    lax.fori_loop(0, 8, taps_grad(xb, gzb, gkb), 0)

    for m, ref in enumerate((gwi, gwoT)):
        for rt in range(12):
            for lt in range(6):
                pay[m * 72 + rt * 6 + lt] = ref[rt * 16 : rt * 16 + 16, lt * 128 : lt * 128 + 128].astype(BF16)
    sum_a = jnp.sum(gka[...], axis=1)
    sum_b = jnp.sum(gkb[...], axis=1)
    sum_b = sum_b + pltpu.roll(sum_b, 64, 1)
    for m in range(4):
        pay[144 + m] = sum_a[m * 16 : m * 16 + 16].astype(BF16)
        pay[148 + m] = sum_b[m * 16 : m * 16 + 16].astype(BF16)
    pay[152:160] = jnp.zeros((8, 16, 128), BF16)

    core_copy = remote(pay.at[pl.ds((1 - core) * 80, 80)], r0, core_sem.at[0], core_sem.at[1], partner, t)
    core_copy.start()

    @pl.when(has_up)
    def _():
        gz_down.wait_recv()

    @pl.when(t == 0)
    def _():
        halo[0] = jnp.zeros((3, 256, 192), BF16)

    @pl.when(has_down)
    def _():
        gz_up.wait_recv()

    @pl.when(t == 31)
    def _():
        halo[1] = jnp.zeros((3, 256, 192), BF16)

    def lay_halo(r, _):
        lay_out(r, gza, gzb, halo[0, r].astype(F32))
        lay_out(r + 11, gza, gzb, halo[1, r].astype(F32))
        return 0

    lax.fori_loop(0, 3, lay_halo, 0)

    def back_a(n, _):
        start = pl.multiple_of(n * 16, 16)
        sums = conv_block(gza, ka, start, True)
        for i in range(8):
            gia[i, pl.ds(start, 16), :] = sums[i]
        return 0

    def back_b(n, _):
        start = pl.multiple_of(n * 16, 16)
        sums = conv_block(gzb, kb, start, True)
        for i in range(8):
            gib[i, pl.ds(start, 16), :] = sums[i]
            gib[i, pl.ds(start + 128, 16), :] = pltpu.roll(sums[i], 64, 1)
        return 0

    def add_tiles(count, dst, first, firsts_at, others):
        def step(n, _):
            total = first[firsts_at + n].astype(F32)
            for ref in others:
                total = total + ref[n].astype(F32)
            dst[n] = total.astype(BF16)
            return 0

        lax.fori_loop(0, count, step, 0)

    core_copy.wait()
    add_tiles(80, s1, pay, core * 80, [r0])
    x_copies = [
        remote(s1.at[pl.ds(((x + d + 1) % 4) * 20, 20)], r1.at[d], x_send.at[d], x_recv.at[d], *x_peers[d]) for d in range(3)
    ]
    for c in x_copies:
        c.start()
    lax.fori_loop(0, 8, back_a, 0)
    for c in x_copies:
        c.wait()
    add_tiles(20, s2, s1, x * 20, [r1.at[d] for d in range(3)])
    y_copies = [
        remote(s2.at[pl.ds(((y + d + 1) % 4) * 5, 5)], r2.at[d], y_send.at[d], y_recv.at[d], *y_peers[d]) for d in range(3)
    ]
    for c in y_copies:
        c.start()
    lax.fori_loop(8, 13, back_a, 0)
    for c in y_copies:
        c.wait()
    add_tiles(5, s3, s2, y * 5, [r2.at[d] for d in range(3)])
    z_copies = [remote(s3, r3.at[z], z_send.at[d], z_recv.at[d], *z_peers[d]) for d in range(3)]
    for c in z_copies:
        c.start()
    r3[z] = s3[...]
    lax.fori_loop(13, 16, back_a, 0)
    for c in z_copies:
        c.wait()
    at_y = core * 80 + x * 20 + y * 5
    total = r3[0].astype(F32)
    for k in range(1, 4):
        total = total + r3[k].astype(F32)
    full[pl.ds(at_y, 5)] = total.astype(BF16)
    y_back = [
        remote(full.at[pl.ds(at_y, 5)], full.at[pl.ds(at_y, 5)], y_send.at[d + 3], y_recv.at[d + 3], *y_peers[d]) for d in range(3)
    ]
    for c in y_back:
        c.start()
    lax.fori_loop(0, 4, back_b, 0)
    for c in y_back:
        c.wait()
    at_x = core * 80 + x * 20
    x_back = [
        remote(full.at[pl.ds(at_x, 20)], full.at[pl.ds(at_x, 20)], x_send.at[d + 3], x_recv.at[d + 3], *x_peers[d]) for d in range(3)
    ]
    for c in x_back:
        c.start()
    lax.fori_loop(4, 8, back_b, 0)

    def back_out(i, _):
        g = ct[i].astype(F32)
        fx[i, :, 0:128] = (g[:, 0:128] + gia[i]).astype(BF16)
        fx[i, :, 128:192] = (g[:, 128:192] + gib[i][:, 0:64]).astype(BF16)
        return 0

    lax.fori_loop(0, 8, back_out, 0)
    gin_out = pltpu.make_async_copy(fx.at[pl.ds(0, 8)], out_gin.at[0, 0], out_sem.at[1])
    gin_out.start()
    for c in x_back:
        c.wait()
    mine = pl.ds(core * 80, 80)
    core_back = remote(full.at[mine], full.at[mine], core_sem.at[2], core_sem.at[3], partner, t)
    core_back.start()
    core_back.wait()

    for m, ref in enumerate((out_gwi, out_gwoT)):
        for rt in range(12):
            for lt in range(6):
                ref[rt * 16 : rt * 16 + 16, lt * 128 : lt * 128 + 128] = full[m * 72 + rt * 6 + lt].astype(F32) * PIXEL_SCALE
    for m in range(4):
        out_gk[m * 16 : m * 16 + 16, 0:128] = full[144 + m].astype(F32) * PIXEL_SCALE
        out_gk[m * 16 : m * 16 + 16, 128:256] = full[148 + m].astype(F32) * PIXEL_SCALE

    @pl.when(has_up)
    def _():
        to_up.wait_send()
        gz_up.wait_send()

    @pl.when(has_down)
    def _():
        to_down.wait_send()
        gz_down.wait_send()

    block_out.wait()
    gin_out.wait()


def on_device(features, dw_kernel, dw_bias, ln_gain, ln_bias, w_in, b_in, w_out, b_out, layer_scale, cotangent):
    row = lambda v: v.reshape(1, -1)
    any_, vmem = pl.BlockSpec(memory_space=pl.ANY), pl.BlockSpec(memory_space=pltpu.VMEM)
    V, DMA = pltpu.VMEM, pltpu.SemaphoreType.DMA
    scratch = [
        V((14, 256, 192), BF16), V((8, 256, 192), BF16),
        V((14, 272, 128), F32), V((14, 144, 128), F32), V((49, 8, 128), F32), V((49, 8, 128), F32),
        V((8, 256, 128), F32), V((8, 256, 128), F32), V((14, 272, 128), F32), V((14, 144, 128), F32),
        V((8, 256), F32), V((256, 768), BF16), V((768, 256), BF16), V((8, 256, 256), BF16), V((8, 192, 256), BF16),
        V((256, 256), BF16), V((256, 256), F32), V((256, 128), F32), V((256, 768), F32), V((256, 768), F32),
        V((256, 768), BF16), V((256, 768), BF16), V((8, 256, 192), BF16), V((8, 256, 192), BF16),
        V((192, 768), F32), V((192, 768), F32), V((64, 8, 128), F32), V((64, 8, 128), F32),
        V((8, 256, 128), F32), V((8, 256, 128), F32),
        V((TILES, 16, 128), BF16), V((80, 16, 128), BF16), V((80, 16, 128), BF16), V((3, 20, 16, 128), BF16),
        V((20, 16, 128), BF16), V((3, 5, 16, 128), BF16), V((5, 16, 128), BF16), V((4, 5, 16, 128), BF16),
        V((TILES, 16, 128), BF16), V((2, 3, 256, 192), BF16),
        DMA((2,)), DMA((2,)), DMA((4,)), DMA((4,)), DMA((4,)), DMA((6,)), DMA((6,)), DMA((6,)), DMA((6,)), DMA((3,)), DMA((3,)),
    ]
    block, gin, gwi, gwoT, gk = pl.pallas_call(
        kernel,
        out_shape=(
            jax.ShapeDtypeStruct((1, 1, 8, 256, 192), BF16), jax.ShapeDtypeStruct((1, 1, 8, 256, 192), BF16),
            jax.ShapeDtypeStruct((192, 768), F32), jax.ShapeDtypeStruct((192, 768), F32), jax.ShapeDtypeStruct((64, 256), F32),
        ),
        in_specs=[any_, any_] + [vmem] * 9,
        out_specs=(any_, any_, vmem, vmem, vmem),
        scratch_shapes=scratch,
        compiler_params=pltpu.CompilerParams(collective_id=0, has_side_effects=True, vmem_limit_bytes=60 << 20),
    )(
        features, cotangent, dw_kernel, row(dw_bias), row(ln_gain), row(ln_bias), w_in, row(b_in), w_out, row(b_out),
        row(layer_scale),
    )
    return block, gin, gwi, gwoT.T, gk[:49, :192].reshape(7, 7, 192)


def solution(mesh):
    split, whole = P("slide", "space", None, None, None), P()
    return jax.shard_map(
        on_device,
        mesh=mesh,
        in_specs=(split,) + (whole,) * 9 + (split,),
        out_specs=(split, split, whole, whole, whole),
        check_vma=False,
    )
```

profile of v0, /device:TPU:1, one launch (start us, length us, event | category | flops | bytes accessed | tf_op | source)
XLA Modules:
  0.0 119.9 jit_solution(5835059697335863207)
XLA Ops:
  0.6 0.0 copy-start.5
  0.6 0.7 copy-done.5
  1.3 0.6 reshape.34.b_in
  1.9 1.9 %copy.18.w_out = bf16[768,192]{1,0:T(8,128)(2,1)} copy(bf16[768,192]{0,1:T(8,128)(2,1)} %param.18) | data formatting | bytes 589824 | tf_op args[7]
  3.8 0.0 copy-start.1
  3.8 2.3 %copy.16.feat = bf16[1,1,8,256,192]{4,3,2,1,0:T(8,128)(2,1)} copy(bf16[1,1,8,256,192]{3,4,2,1,0:T(8,128)(2,1)} %param.11) | data formatting | bytes 1572864 | tf_op args[0]
  6.1 0.0 copy-done.1
  6.1 1.3 %copy.17.cot = bf16[1,1,8,256,192]{4,3,2,1,0:T(8,128)(2,1)} copy(bf16[1,1,8,256,192]{3,4,2,1,0:T(8,128)(2,1)S(1)} %copy-done.1) | data formatting | bytes 1572864 | tf_op args[10]
  7.4 106.2 %shard_map.146 = (bf16[1,1,8,256,192]{4,3,2,1,0:T(8,128)(2,1)}, bf16[1,1,8,256,192]{4,3,2,1,0:T(8,128)(2,1)}, f32[192,768]{1,0:T(8,128)}, f32[192,768]{1,0:T(8,128)}, f32[64,256]{1,0:T(8,128)}) custom-call(bf16[1,1,8,256,192]{4,3,2,1,0:T(8,128)(2,1)} %copy.16.feat, bf16[1,1,8,256,192]{4,3,2,1,0:T(8,128)(2,1)} %copy.17.cot, f32[7,7,192]{2,1,0:T(8,128)} %dwk.1, ...), custom_call_target="tpu_custom_call" | custom-call | tf_op jit(solution)/shard_map/pallas_call | solution.py:440
  113.6 0.0 copy-start
  113.6 0.0 copy-start.4
  113.6 2.3 %copy.19 = bf16[1,1,8,256,192]{3,4,2,1,0:T(8,128)(2,1)} copy(bf16[1,1,8,256,192]{4,3,2,1,0:T(8,128)(2,1)} %get-tuple-element.15) | data formatting | bytes 1572864
  115.9 0.0 copy-done.4
  115.9 0.6 reshape.37
  116.5 0.0 copy-done
  116.5 0.0 copy-start.3
  116.5 1.3 %copy.20 = bf16[1,1,8,256,192]{3,4,2,1,0:T(8,128)(2,1)} copy(bf16[1,1,8,256,192]{4,3,2,1,0:T(8,128)(2,1)S(1)} %copy-done) | data formatting | bytes 1572864
  117.8 0.0 copy-done.3
  117.8 0.0 copy-start.2
  117.8 0.8 copy.23
  118.6 0.5 copy-done.2
  119.1 0.8 copy.24
  (1 shorter events, 0.0 us)
Async XLA Ops:
  0.6 0.7 copy-start.5
  3.8 2.3 %copy-start.1 = (bf16[1,1,8,256,192]{3,4,2,1,0:T(8,128)(2,1)S(1)}, bf16[1,1,8,256,192]{3,4,2,1,0:T(8,128)(2,1)}, u32[]{:S(2)}) copy-start(bf16[1,1,8,256,192]{3,4,2,1,0:T(8,128)(2,1)} %param.21) | copy-start | bytes 2359300
  113.6 3.0 %copy-start = (bf16[1,1,8,256,192]{4,3,2,1,0:T(8,128)(2,1)S(1)}, bf16[1,1,8,256,192]{4,3,2,1,0:T(8,128)(2,1)}, u32[]{:S(2)}) copy-start(bf16[1,1,8,256,192]{4,3,2,1,0:T(8,128)(2,1)} %get-tuple-element.16) | copy-start | bytes 2359300
  113.6 2.3 %copy-start.4 = (f32[64,256]{1,0:T(8,128)S(1)}, f32[64,256]{1,0:T(8,128)}, u32[]{:S(2)}) copy-start(f32[64,256]{1,0:T(8,128)} %get-tuple-element.14) | copy-start | bytes 196612
  116.5 1.3 %copy-start.3 = (f32[192,768]{1,0:T(8,128)S(1)}, f32[192,768]{1,0:T(8,128)}, u32[]{:S(2)}) copy-start(f32[192,768]{1,0:T(8,128)} %get-tuple-element.27) | copy-start | bytes 1769476
  117.8 1.3 %copy-start.2 = (f32[192,768]{1,0:T(8,128)S(1)}, f32[192,768]{1,0:T(8,128)}, u32[]{:S(2)}) copy-start(f32[192,768]{1,0:T(8,128)} %get-tuple-element.13) | copy-start | bytes 1769476
where the time goes:
time: 120 us
  Pallas kernels  106 us (88%)
  local copies, waits for them, and re-layouts  13.1 us (11%)
    pallas_call x1, Pallas kernels, on_device(): pl.pallas_call(kernel, out_shape=(jax.ShapeDtypeStruct((1, 1, 8, 256, 192...  106 us
    unnamed x19, local copies, waits for them, and re-layouts  11.8 us

commit v1 on v0

v1 whole, which is shorter than its diff:
```python
import jax
import jax.numpy as jnp
from jax import lax
from jax.experimental import pallas as pl
from jax.experimental.pallas import tpu as pltpu
from jax.sharding import PartitionSpec as P

EPSILON = 1e-06
F32 = jnp.float32
BF16 = jnp.bfloat16
MESH = pl.DeviceIdType.MESH
PIXEL_SCALE = float(262144) ** (-0.5)
TILES = 160
NT = (((1,), (1,)), ((), ()))


def remote(src, dst, send, recv, slide, space):
    return pltpu.make_async_remote_copy(
        src_ref=src, dst_ref=dst, send_sem=send, recv_sem=recv,
        device_id={"slide": slide, "space": space}, device_id_type=MESH,
    )


def gelu_parts(h):
    cdf = 0.5 * (1.0 + lax.erf(h * 0.7071067811865476))
    slope = cdf + h * jnp.exp(-0.5 * h * h) * 0.3989422804014327
    return h * cdf, slope


def spread(value, row, group, dst):
    column = lax.broadcasted_iota(jnp.int32, (16, 256), 1)
    wide = value.astype(F32)
    for b in range(7):
        moved = wide
        if b != 3:
            moved = pltpu.roll(wide, (3 - b) % 256, 1)
            inside = column >= 3 - b if b < 3 else column < 259 - b
            moved = jnp.where(inside, moved, 0.0)
        dst[group, pl.ds(pl.multiple_of((b * 16 + row) * 16, 16), 16), :] = moved.astype(BF16)


def build_taps(dwk, flat, taps, flip):
    lane8 = lax.broadcasted_iota(jnp.int32, (8, 128), 1)
    for a in range(7):
        flat[a, 0:7, 0:192] = jnp.concatenate(
            [dwk[6 - a if flip else a, (6 - b if flip else b) : (6 - b if flip else b) + 1, :] for b in range(7)], axis=0
        )
    for g in range(12):
        base = jnp.zeros((8, 128), F32)
        tile, at = g // 8 * 128, g % 8 * 16
        for a in range(7):
            v = flat[a, :, tile : tile + 128]
            v = pltpu.roll(v, (a * 16 - at) % 128, 1)
            base = jnp.where((lane8 >= a * 16) & (lane8 < a * 16 + 16), v, base)
        flat[7 + g, :, 0:128] = base
    same = (
        lax.broadcasted_iota(jnp.int32, (16, 128), 1) % 16 == lax.broadcasted_iota(jnp.int32, (16, 128), 0)
    )

    def group(g, _):
        base = flat[7 + g, :, 0:128]
        for i in range(8):
            moved = pltpu.roll(base, i * 16, 1) if i else base
            first = jnp.where(lane8 >= i * 16, moved, 0.0)
            second = jnp.where(lane8 < i * 16, moved, 0.0)
            for b in range(7):
                for half, v in enumerate((first, second)):
                    row = jnp.broadcast_to(v[b : b + 1, :], (16, 128))
                    taps[g, i * 16 : i * 16 + 16, b * 256 + half * 128 : b * 256 + half * 128 + 128] = jnp.where(
                        same, row, 0.0
                    ).astype(BF16)
        return 0

    lax.fori_loop(0, 12, group, 0)


def kernel(
    feat, cot, dwk, dwb, gain, lbias, w_in, b_in, woutT, b_out, lscale,
    out_block, out_gin, out_gwi, out_gwoT, out_gk,
    fx, ct, xs, gs, taps, back, flat, zf, par, bias, winT, wout, gout,
    nb, unit, hid, gact, act, gh, outs, gzs, gwi, gwoT, gkr,
    pay, r0, s1, r1, s2, r2, s3, r3, full, halo,
    in_sem, out_sem, halo_send, halo_recv, core_sem, x_send, x_recv, y_send, y_recv, z_send, z_recv,
):
    s, t = lax.axis_index("slide"), lax.axis_index("space")
    z_hi, core = s // 2, s % 2
    z_lo, x, y = t % 2, (t // 2) % 4, t // 8
    z = z_hi * 2 + z_lo
    partner = z_hi * 2 + (1 - core)
    x_peers = [(s, (y * 4 + (x + d) % 4) * 2 + z_lo) for d in (1, 2, 3)]
    y_peers = [(s, (((y + d) % 4) * 4 + x) * 2 + z_lo) for d in (1, 2, 3)]
    z_peers = [(((z + d) % 4) // 2 * 2 + core, (y * 4 + x) * 2 + ((z + d) % 4) % 2) for d in (1, 2, 3)]
    has_up, has_down = t > 0, t < 31
    up, down = jnp.maximum(t - 1, 0), jnp.minimum(t + 1, 31)

    barrier = pltpu.get_barrier_semaphore()
    for ps, pt in [(partner, t)] + x_peers + y_peers + z_peers:
        pl.semaphore_signal(barrier, inc=1, device_id={"slide": ps, "space": pt}, device_id_type=MESH)

    @pl.when(has_up)
    def _():
        pl.semaphore_signal(barrier, inc=1, device_id={"slide": s, "space": up}, device_id_type=MESH)

    @pl.when(has_down)
    def _():
        pl.semaphore_signal(barrier, inc=1, device_id={"slide": s, "space": down}, device_id_type=MESH)

    own_in = pltpu.make_async_copy(feat.at[0, 0], fx.at[pl.ds(3, 8)], in_sem.at[0])
    own_in.start()
    cot_in = pltpu.make_async_copy(cot.at[0, 0], ct, in_sem.at[1])
    cot_in.start()

    pl.semaphore_wait(barrier, 10 + jnp.minimum(t, 1) + jnp.minimum(31 - t, 1))

    to_up = remote(feat.at[0, 0, pl.ds(0, 3)], fx.at[pl.ds(11, 3)], halo_send.at[0], halo_recv.at[0], s, up)
    to_down = remote(feat.at[0, 0, pl.ds(5, 3)], fx.at[pl.ds(0, 3)], halo_send.at[1], halo_recv.at[1], s, down)

    @pl.when(has_up)
    def _():
        to_up.start()

    @pl.when(has_down)
    def _():
        to_down.start()

    for n, ref in enumerate((dwb, gain, lbias, b_out, lscale)):
        par[n, 0:128, :] = jnp.broadcast_to(ref[:, 0:128], (128, 128)).T
        tail = jnp.concatenate([ref[:, 128:192], ref[:, 128:192]], axis=1)
        par[n, 128:256, :] = jnp.broadcast_to(tail, (128, 128)).T
    for n in range(6):
        bias[n * 128 : n * 128 + 128, :] = jnp.broadcast_to(b_in[:, n * 128 : n * 128 + 128], (128, 128)).T
    winT[...] = w_in[...].T
    wout[...] = woutT[...].T
    gwi[...] = jnp.zeros_like(gwi)
    gwoT[...] = jnp.zeros_like(gwoT)

    def clear(g, _):
        none = jnp.zeros((32, 256), BF16)
        for b in range(7):
            xs[g, b * 256 + 224 : b * 256 + 256, :] = none
            gs[g, b * 256 + 224 : b * 256 + 256, :] = none
        return 0

    lax.fori_loop(0, 12, clear, 0)
    build_taps(dwk, flat, taps, False)
    build_taps(dwk, flat, back, True)

    cot_in.wait()

    def both(v):
        return jnp.concatenate([v, v], axis=1)

    def scale_row(i, _):
        gout[i] = (both(par[4, 0:192, :]) * ct[i].astype(F32)).astype(BF16)
        return 0

    lax.fori_loop(0, 8, scale_row, 0)
    own_in.wait()

    @pl.when(has_up)
    def _():
        to_down.wait_recv()

    @pl.when(t == 0)
    def _():
        fx[0:3] = jnp.zeros((3, 192, 256), BF16)

    @pl.when(has_down)
    def _():
        to_up.wait_recv()

    @pl.when(t == 31)
    def _():
        fx[11:14] = jnp.zeros((3, 192, 256), BF16)

    def group_rows(g):
        return pl.ds(pl.multiple_of(g * 16, 16), 16)

    def spread_x(n, _):
        r, g = n // 12, n % 12
        spread(fx[r, group_rows(g), :], r, g, xs)
        return 0

    lax.fori_loop(0, 14 * 12, spread_x, 0)

    def conv(g, _):
        z = jnp.dot(taps[g], xs[g], preferred_element_type=F32)
        for i in range(8):
            zf[i, group_rows(g), :] = z[i * 16 : i * 16 + 16, :] + both(par[0, group_rows(g), :])
        return 0

    lax.fori_loop(0, 12, conv, 0)

    def mlp_row(i, _):
        def norm(q, _):
            ln = pl.ds(pl.multiple_of(q * 128, 128), 128)
            v = zf[i, :, ln]
            v = v - jnp.sum(v, axis=0, keepdims=True) * (1.0 / 192)
            var = jnp.sum(v * v, axis=0, keepdims=True) * (1.0 / 192)
            r = lax.rsqrt(var + EPSILON)
            v = v * r
            zf[i, :, ln] = v
            unit[0:8, ln] = jnp.broadcast_to(r, (8, 128))
            nb[:, ln] = (v * par[1, 0:192, :] + par[2, 0:192, :]).astype(BF16)
            return 0

        lax.fori_loop(0, 2, norm, 0)
        hid[...] = jnp.dot(winT[...], nb[...], preferred_element_type=F32)
        gact[...] = jnp.dot(wout[...], gout[i], preferred_element_type=F32)

        def gelu(n, _):
            px = pl.ds(pl.multiple_of(n * 16, 16), 16)
            value, slope = gelu_parts(hid[px, :] + both(bias[px, :]))
            act[px, :] = value.astype(BF16)
            gh[px, :] = (gact[px, :] * slope).astype(BF16)
            return 0

        lax.fori_loop(0, 48, gelu, 0)
        hid[0:192, :] = jnp.dot(woutT[...], act[...], preferred_element_type=F32)
        hid[192:384, :] = jnp.dot(w_in[...], gh[...], preferred_element_type=F32)
        gwi[...] += lax.dot_general(nb[...], gh[...], NT, preferred_element_type=F32)
        gwoT[...] += lax.dot_general(gout[i], act[...], NT, preferred_element_type=F32)

        def finish(q, _):
            ln = pl.ds(pl.multiple_of(q * 128, 128), 128)
            branch = hid[0:192, ln] + par[3, 0:192, :]
            outs[i, :, ln] = (fx[i + 3, :, ln].astype(F32) + par[4, 0:192, :] * branch).astype(BF16)
            gn = hid[192:384, ln] * par[1, 0:192, :]
            u = zf[i, :, ln]
            m1 = jnp.sum(gn, axis=0, keepdims=True) * (1.0 / 192)
            m2 = jnp.sum(gn * u, axis=0, keepdims=True) * (1.0 / 192)
            gzs[i, :, ln] = (unit[0:1, ln] * (gn - m1 - u * m2)).astype(BF16)
            return 0

        lax.fori_loop(0, 2, finish, 0)

        def spread_gz(g, _):
            spread(gzs[i, group_rows(g), :], i + 3, g, gs)
            return 0

        lax.fori_loop(0, 12, spread_gz, 0)
        return 0

    lax.fori_loop(0, 8, mlp_row, 0)
    block_out = pltpu.make_async_copy(outs, out_block.at[0, 0], out_sem.at[0])
    block_out.start()

    gz_up = remote(gzs.at[pl.ds(0, 3)], halo.at[1], halo_send.at[2], halo_recv.at[2], s, up)
    gz_down = remote(gzs.at[pl.ds(5, 3)], halo.at[0], halo_send.at[3], halo_recv.at[3], s, down)

    @pl.when(has_up)
    def _():
        gz_up.start()

    @pl.when(has_down)
    def _():
        gz_down.start()

    same = lax.broadcasted_iota(jnp.int32, (16, 256), 1) % 16 == lax.broadcasted_iota(jnp.int32, (16, 256), 0)
    lane8 = lax.broadcasted_iota(jnp.int32, (8, 128), 1)

    def taps_grad(g, _):
        own = gs[g, 3 * 256 + 48 : 3 * 256 + 48 + 128, :]
        for b in range(7):
            pairs = lax.dot_general(own, xs[g, b * 256 : b * 256 + 256, :], NT, preferred_element_type=F32)
            total = jnp.zeros((8, 128), F32)
            for i in range(8):
                v = jnp.where(same, pairs[i * 16 : i * 16 + 16, :], 0.0)
                v = v[0:8] + v[8:16]
                if i == 0:
                    total = total + v[:, 0:128]
                else:
                    v = pltpu.roll(jnp.where(lane8 >= i * 16, v[:, 0:128], v[:, 128:256]), 128 - i * 16, 1)
                    total = total + v
            gkr[g, b : b + 1, :] = jnp.sum(total, axis=0, keepdims=True)
        gkr[g, 7:8, :] = jnp.zeros((1, 128), F32)
        return 0

    lax.fori_loop(0, 12, taps_grad, 0)

    for m, ref in enumerate((gwi, gwoT)):
        for rt in range(12):
            for lt in range(6):
                pay[m * 72 + rt * 6 + lt] = ref[rt * 16 : rt * 16 + 16, lt * 128 : lt * 128 + 128].astype(BF16)
    for m in range(6):
        pay[144 + m] = jnp.concatenate([gkr[2 * m], gkr[2 * m + 1]], axis=0).astype(BF16)
    pay[150:160] = jnp.zeros((10, 16, 128), BF16)

    core_copy = remote(pay.at[pl.ds((1 - core) * 80, 80)], r0, core_sem.at[0], core_sem.at[1], partner, t)
    core_copy.start()

    @pl.when(has_up)
    def _():
        gz_down.wait_recv()

    @pl.when(t == 0)
    def _():
        halo[0] = jnp.zeros((3, 192, 256), BF16)

    @pl.when(has_down)
    def _():
        gz_up.wait_recv()

    @pl.when(t == 31)
    def _():
        halo[1] = jnp.zeros((3, 192, 256), BF16)

    def spread_halo(n, _):
        r, g = n // 12, n % 12
        spread(halo[0, r, group_rows(g), :], r, g, gs)
        spread(halo[1, r, group_rows(g), :], r + 11, g, gs)
        return 0

    lax.fori_loop(0, 36, spread_halo, 0)

    def back_conv(g, _):
        v = jnp.dot(back[g], gs[g], preferred_element_type=F32)
        for i in range(8):
            fx[i, group_rows(g), :] = (ct[i, group_rows(g), :].astype(F32) + v[i * 16 : i * 16 + 16, :]).astype(BF16)
        return 0

    def add_tiles(count, dst, first, firsts_at, others):
        def step(n, _):
            total = first[firsts_at + n].astype(F32)
            for ref in others:
                total = total + ref[n].astype(F32)
            dst[n] = total.astype(BF16)
            return 0

        lax.fori_loop(0, count, step, 0)

    core_copy.wait()
    add_tiles(80, s1, pay, core * 80, [r0])
    x_copies = [
        remote(s1.at[pl.ds(((x + d + 1) % 4) * 20, 20)], r1.at[d], x_send.at[d], x_recv.at[d], *x_peers[d]) for d in range(3)
    ]
    for c in x_copies:
        c.start()
    lax.fori_loop(0, 4, back_conv, 0)
    for c in x_copies:
        c.wait()
    add_tiles(20, s2, s1, x * 20, [r1.at[d] for d in range(3)])
    y_copies = [
        remote(s2.at[pl.ds(((y + d + 1) % 4) * 5, 5)], r2.at[d], y_send.at[d], y_recv.at[d], *y_peers[d]) for d in range(3)
    ]
    for c in y_copies:
        c.start()
    lax.fori_loop(4, 6, back_conv, 0)
    for c in y_copies:
        c.wait()
    add_tiles(5, s3, s2, y * 5, [r2.at[d] for d in range(3)])
    z_copies = [remote(s3, r3.at[z], z_send.at[d], z_recv.at[d], *z_peers[d]) for d in range(3)]
    for c in z_copies:
        c.start()
    r3[z] = s3[...]
    lax.fori_loop(6, 8, back_conv, 0)
    for c in z_copies:
        c.wait()
    at_y = core * 80 + x * 20 + y * 5
    total = r3[0].astype(F32)
    for k in range(1, 4):
        total = total + r3[k].astype(F32)
    full[pl.ds(at_y, 5)] = total.astype(BF16)
    y_back = [
        remote(full.at[pl.ds(at_y, 5)], full.at[pl.ds(at_y, 5)], y_send.at[d + 3], y_recv.at[d + 3], *y_peers[d]) for d in range(3)
    ]
    for c in y_back:
        c.start()
    lax.fori_loop(8, 10, back_conv, 0)
    for c in y_back:
        c.wait()
    at_x = core * 80 + x * 20
    x_back = [
        remote(full.at[pl.ds(at_x, 20)], full.at[pl.ds(at_x, 20)], x_send.at[d + 3], x_recv.at[d + 3], *x_peers[d]) for d in range(3)
    ]
    for c in x_back:
        c.start()
    lax.fori_loop(10, 12, back_conv, 0)
    gin_out = pltpu.make_async_copy(fx.at[pl.ds(0, 8)], out_gin.at[0, 0], out_sem.at[1])
    gin_out.start()
    for c in x_back:
        c.wait()
    mine = pl.ds(core * 80, 80)
    core_back = remote(full.at[mine], full.at[mine], core_sem.at[2], core_sem.at[3], partner, t)
    core_back.start()
    core_back.wait()

    for m, ref in enumerate((out_gwi, out_gwoT)):
        for rt in range(12):
            for lt in range(6):
                ref[rt * 16 : rt * 16 + 16, lt * 128 : lt * 128 + 128] = full[m * 72 + rt * 6 + lt].astype(F32) * PIXEL_SCALE
    for m in range(6):
        out_gk[m * 16 : m * 16 + 16, :] = full[144 + m].astype(F32) * PIXEL_SCALE

    @pl.when(has_up)
    def _():
        to_up.wait_send()
        gz_up.wait_send()

    @pl.when(has_down)
    def _():
        to_down.wait_send()
        gz_down.wait_send()

    block_out.wait()
    gin_out.wait()


def on_device(features, dw_kernel, dw_bias, ln_gain, ln_bias, w_in, b_in, w_out, b_out, layer_scale, cotangent):
    row = lambda v: v.reshape(1, -1)
    turn = lambda v: jnp.swapaxes(v, 3, 4)
    any_, vmem = pl.BlockSpec(memory_space=pl.ANY), pl.BlockSpec(memory_space=pltpu.VMEM)
    V, DMA = pltpu.VMEM, pltpu.SemaphoreType.DMA
    scratch = [
        V((14, 192, 256), BF16), V((8, 192, 256), BF16), V((12, 1792, 256), BF16), V((12, 1792, 256), BF16),
        V((12, 128, 1792), BF16), V((12, 128, 1792), BF16), V((19, 8, 256), F32), V((8, 192, 256), F32),
        V((5, 256, 128), F32), V((768, 128), F32), V((768, 192), BF16), V((768, 192), BF16), V((8, 192, 256), BF16),
        V((192, 256), BF16), V((8, 256), F32), V((768, 256), F32), V((768, 256), F32), V((768, 256), BF16),
        V((768, 256), BF16), V((8, 192, 256), BF16), V((8, 192, 256), BF16),
        V((192, 768), F32), V((192, 768), F32), V((12, 8, 128), F32),
        V((TILES, 16, 128), BF16), V((80, 16, 128), BF16), V((80, 16, 128), BF16), V((3, 20, 16, 128), BF16),
        V((20, 16, 128), BF16), V((3, 5, 16, 128), BF16), V((5, 16, 128), BF16), V((4, 5, 16, 128), BF16),
        V((TILES, 16, 128), BF16), V((2, 3, 192, 256), BF16),
        DMA((2,)), DMA((2,)), DMA((4,)), DMA((4,)), DMA((4,)), DMA((6,)), DMA((6,)), DMA((6,)), DMA((6,)), DMA((3,)), DMA((3,)),
    ]
    block, gin, gwi, gwoT, gk = pl.pallas_call(
        kernel,
        out_shape=(
            jax.ShapeDtypeStruct((1, 1, 8, 192, 256), BF16), jax.ShapeDtypeStruct((1, 1, 8, 192, 256), BF16),
            jax.ShapeDtypeStruct((192, 768), F32), jax.ShapeDtypeStruct((192, 768), F32), jax.ShapeDtypeStruct((96, 128), F32),
        ),
        in_specs=[any_, any_] + [vmem] * 9,
        out_specs=(any_, any_, vmem, vmem, vmem),
        scratch_shapes=scratch,
        compiler_params=pltpu.CompilerParams(collective_id=0, has_side_effects=True, vmem_limit_bytes=60 << 20),
    )(
        turn(features), turn(cotangent), dw_kernel, row(dw_bias), row(ln_gain), row(ln_bias), w_in, row(b_in), w_out.T, row(b_out),
        row(layer_scale),
    )
    gk = gk.reshape(12, 8, 8, 16)[:, :7, :7].transpose(2, 1, 0, 3).reshape(7, 7, 192)
    return turn(block), turn(gin), gwi, gwoT.T, gk


def solution(mesh):
    split, whole = P("slide", "space", None, None, None), P()
    return jax.shard_map(
        on_device,
        mesh=mesh,
        in_specs=(split,) + (whole,) * 9 + (split,),
        out_specs=(split, split, whole, whole, whole),
        check_vma=False,
    )
```

time: 120 us -> 123 us (1.025)
  Pallas kernels: 106 us -> 113 us
  local copies, waits for them, and re-layouts: 13.1 us -> 8.17 us
    pallas_call x1, Pallas kernels: 106 us -> 113 us  [on_device(): pl.pallas_call(kernel, out_shape=(jax.ShapeDtypeStruct((1, 1, 8, 192, 256...]
    unnamed x19 -> x15, local copies, waits for them, and re-layouts: 11.8 us -> 5.83 us
where the time goes in v1:
time: 123 us; the launch traced here: 122 us
  Pallas kernels  113 us (92%)
  local copies, waits for them, and re-layouts  8.17 us (7%)
    pallas_call x1, Pallas kernels, on_device(): pl.pallas_call(kernel, out_shape=(jax.ShapeDtypeStruct((1, 1, 8, 192, 256...  113 us
    unnamed x15, local copies, waits for them, and re-layouts  5.83 us

profile of v1, /device:TPU:1, one launch (start us, length us, event | category | flops | bytes accessed | tf_op | source)
XLA Modules:
  0.0 122.2 jit_solution(13334233969287386558)
XLA Ops:
  0.6 0.0 copy-start.4
  0.6 0.7 copy-done.4
  1.3 0.6 reshape.37.b_in
  1.9 113.3 %shard_map.146 = (bf16[1,1,8,192,256]{4,3,2,1,0:T(8,128)(2,1)}, bf16[1,1,8,192,256]{4,3,2,1,0:T(8,128)(2,1)}, f32[192,768]{1,0:T(8,128)}, f32[192,768]{1,0:T(8,128)}, f32[96,128]{1,0:T(8,128)}) custom-call(bf16[1,1,8,192,256]{4,3,2,1,0:T(8,128)(2,1)} %bitcast.15, bf16[1,1,8,192,256]{4,3,2,1,0:T(8,128)(2,1)} %bitcast.16, f32[7,7,192]{2,1,0:T(8,128)} %dwk.1, ...), custom_call_target="tpu_custom_call" | custom-call | tf_op jit(solution)/shard_map/pallas_call | solution.py:426
  115.3 1.0 reshape.40
  116.2 0.0 copy-start.1
  116.3 0.1 copy.20
  116.3 0.8 reshape.41
  117.1 0.2 copy-done.1
  117.4 0.0 copy-start
  117.4 0.9 copy.25
  118.2 0.5 copy-done
  118.8 0.0 copy-start.3
  118.8 0.9 copy.26
  119.6 0.5 copy-done.3
  120.1 0.0 copy-start.2
  120.1 0.8 copy.27
  120.9 0.5 copy-done.2
  121.4 0.8 copy.28
  (1 shorter events, 0.0 us)
Async XLA Ops:
  0.6 0.7 copy-start.4
  116.2 1.1 copy-start.1
  117.4 1.4 %copy-start = (bf16[1,1,8,192,256]{4,3,2,1,0:T(8,128)(2,1)S(1)}, bf16[1,1,8,192,256]{4,3,2,1,0:T(8,128)(2,1)}, u32[]{:S(2)}) copy-start(bf16[1,1,8,192,256]{4,3,2,1,0:T(8,128)(2,1)} %get-tuple-element.11) | copy-start | bytes 2359300
  118.8 1.3 %copy-start.3 = (f32[192,768]{1,0:T(8,128)S(1)}, f32[192,768]{1,0:T(8,128)}, u32[]{:S(2)}) copy-start(f32[192,768]{1,0:T(8,128)} %get-tuple-element.22) | copy-start | bytes 1769476
  120.1 1.3 %copy-start.2 = (f32[192,768]{1,0:T(8,128)S(1)}, f32[192,768]{1,0:T(8,128)}, u32[]{:S(2)}) copy-start(f32[192,768]{1,0:T(8,128)} %get-tuple-element.13) | copy-start | bytes 1769476

commit v2 on v1

v2 whole, which is shorter than its diff:
```python
import jax
import jax.numpy as jnp
from jax import lax
from jax.experimental import pallas as pl
from jax.experimental.pallas import tpu as pltpu
from jax.sharding import PartitionSpec as P

EPSILON = 1e-06
F32 = jnp.float32
BF16 = jnp.bfloat16
MESH = pl.DeviceIdType.MESH
PIXEL_SCALE = float(262144) ** (-0.5)
NT = (((1,), (1,)), ((), ()))


def remote(src, dst, send, recv, slide, space):
    return pltpu.make_async_remote_copy(
        src_ref=src, dst_ref=dst, send_sem=send, recv_sem=recv,
        device_id={"slide": slide, "space": space}, device_id_type=MESH,
    )


def gelu_parts(h):
    cdf = 0.5 * (1.0 + lax.erf(h * 0.7071067811865476))
    slope = cdf + h * jnp.exp(-0.5 * h * h) * 0.3989422804014327
    return h * cdf, slope


def spread(value, slot, group, dst):
    lane = lax.broadcasted_iota(jnp.int32, (16, 128), 1)
    left, right = value[:, 0:128], value[:, 128:256]
    none = jnp.zeros_like(left)
    for b in range(7):
        d = b - 3
        first, second = left, right
        if d:
            first, second = pltpu.roll(left, -d % 128, 1), pltpu.roll(right, -d % 128, 1)
            if d > 0:
                first, second = jnp.where(lane < 128 - d, first, second), jnp.where(lane < 128 - d, second, none)
            else:
                first, second = jnp.where(lane < -d, none, first), jnp.where(lane < -d, first, second)
        at = b * 128 + slot * 16
        dst[group, at : at + 16, 0:128] = first
        dst[group, at : at + 16, 128:256] = second


def valid(i, lane):
    slot = lane // 16
    own = (slot >= i - 3) & (slot <= i + 3)
    halo = jnp.zeros_like(own)
    if i < 3:
        halo = slot >= i + 5
    if i >= 5:
        halo = slot <= i - 5
    return own, halo


def build_taps(dwk, flat, own, halo, flip):
    lane8 = lax.broadcasted_iota(jnp.int32, (8, 128), 1)
    for a in range(7):
        flat[a, 0:7, 0:192] = jnp.concatenate(
            [dwk[6 - a if flip else a, (6 - b if flip else b) : (6 - b if flip else b) + 1, :] for b in range(7)], axis=0
        )
    for g in range(12):
        base = jnp.zeros((8, 128), F32)
        tile, at = g // 8 * 128, g % 8 * 16
        for a in range(7):
            v = flat[a, :, tile : tile + 128]
            v = pltpu.roll(v, (a * 16 - at) % 128, 1)
            base = jnp.where((lane8 >= a * 16) & (lane8 < a * 16 + 16), v, base)
        flat[7 + g, :, 0:128] = base
    lane = lax.broadcasted_iota(jnp.int32, (16, 128), 1)
    same = lane % 16 == lax.broadcasted_iota(jnp.int32, (16, 128), 0)

    def group(g, _):
        base = flat[7 + g, :, 0:128]
        for i in range(8):
            moved = pltpu.roll(base, (i - 3) * 16 % 128, 1)
            for keep, dst in zip(valid(i, lane8), (own, halo)):
                if dst is halo and 3 <= i < 5:
                    dst[g, i * 16 : i * 16 + 16, :] = jnp.zeros((16, 896), BF16)
                    continue
                v = jnp.where(keep, moved, 0.0)
                for b in range(7):
                    row = jnp.broadcast_to(v[b : b + 1, :], (16, 128))
                    dst[g, i * 16 : i * 16 + 16, b * 128 : b * 128 + 128] = jnp.where(same, row, 0.0).astype(BF16)
        return 0

    lax.fori_loop(0, 12, group, 0)


def both(v):
    return jnp.concatenate([v, v], axis=1)


def rows16(g):
    return pl.ds(pl.multiple_of(g * 16, 16), 16)


HALO_SLOTS = ((0, 5), (1, 6), (2, 7), (11, 0), (12, 1), (13, 2))


def kernel(
    feat, cot, dwk, dwb, gain, lbias, w_in, b_in, woutT, b_out, lscale,
    out_block, out_gin, out_gwi, out_gwoT, out_gk,
    fx, ct, xs, xh, gs, gh_, taps, taps_h, back, back_h, flat, zf, par, bias, winT, wout, gout,
    nb, rinv, osum, nsum, outs, gzs, gw, gkr, halo,
    pay, r0, s1f, s1b, r1, ry, rz, full, k0, kx, ky, kz, kfull,
    in_sem, out_sem, halo_send, halo_recv, ar_send, ar_recv, k_send, k_recv,
):
    s, t = lax.axis_index("slide"), lax.axis_index("space")
    z_hi, core = s // 2, s % 2
    z_lo, x, y = t % 2, (t // 2) % 4, t // 8
    z = z_hi * 2 + z_lo
    partner = z_hi * 2 + (1 - core)
    x_peers = [(s, (y * 4 + (x + d) % 4) * 2 + z_lo) for d in (1, 2, 3)]
    y_peers = [(s, (((y + d) % 4) * 4 + x) * 2 + z_lo) for d in (1, 2, 3)]
    z_peers = [(((z + d) % 4) // 2 * 2 + core, (y * 4 + x) * 2 + ((z + d) % 4) % 2) for d in (1, 2, 3)]
    has_up, has_down = t > 0, t < 31
    up, down = jnp.maximum(t - 1, 0), jnp.minimum(t + 1, 31)

    own_in = pltpu.make_async_copy(feat.at[0, 0], fx.at[pl.ds(3, 8)], in_sem.at[0])
    own_in.start()
    cot_in = pltpu.make_async_copy(cot.at[0, 0], ct, in_sem.at[1])
    cot_in.start()

    barrier = pltpu.get_barrier_semaphore()
    for ps, pt in [(partner, t)] + x_peers + y_peers + z_peers:
        pl.semaphore_signal(barrier, inc=1, device_id={"slide": ps, "space": pt}, device_id_type=MESH)

    @pl.when(has_up)
    def _():
        pl.semaphore_signal(barrier, inc=1, device_id={"slide": s, "space": up}, device_id_type=MESH)

    @pl.when(has_down)
    def _():
        pl.semaphore_signal(barrier, inc=1, device_id={"slide": s, "space": down}, device_id_type=MESH)

    pl.semaphore_wait(barrier, 10 + jnp.minimum(t, 1) + jnp.minimum(31 - t, 1))

    to_up = remote(feat.at[0, 0, pl.ds(0, 3)], fx.at[pl.ds(11, 3)], halo_send.at[0], halo_recv.at[0], s, up)
    to_down = remote(feat.at[0, 0, pl.ds(5, 3)], fx.at[pl.ds(0, 3)], halo_send.at[1], halo_recv.at[1], s, down)

    @pl.when(has_up)
    def _():
        to_up.start()

    @pl.when(has_down)
    def _():
        to_down.start()

    for n, ref in enumerate((dwb, gain, lbias, b_out, lscale)):
        par[n, 0:128, :] = jnp.broadcast_to(ref[:, 0:128], (128, 128)).T
        par[n, 128:256, :] = jnp.broadcast_to(both(ref[:, 128:192]), (128, 128)).T
    for n in range(6):
        bias[n * 128 : n * 128 + 128, :] = jnp.broadcast_to(b_in[:, n * 128 : n * 128 + 128], (128, 128)).T
    winT[...] = w_in[...].T
    wout[...] = woutT[...].T
    build_taps(dwk, flat, taps, taps_h, False)

    def clear(g, _):
        none = jnp.zeros((32, 256), BF16)
        for b in range(7):
            xh[g, b * 128 + 48 : b * 128 + 80, :] = none
            gh_[g, b * 128 + 48 : b * 128 + 80, :] = none
        return 0

    lax.fori_loop(0, 12, clear, 0)
    own_in.wait()

    def conv_own(g, _):
        for i in range(8):
            spread(fx[i + 3, rows16(g), :], i, g, xs)
        v = jnp.dot(taps[g], xs[g], preferred_element_type=F32)
        for i in range(8):
            zf[i, rows16(g), :] = v[i * 16 : i * 16 + 16, :] + both(par[0, rows16(g), :])
        return 0

    lax.fori_loop(0, 12, conv_own, 0)
    build_taps(dwk, flat, back, back_h, True)
    cot_in.wait()

    def scale_row(i, _):
        gout[i] = (both(par[4, 0:192, :]) * ct[i].astype(F32)).astype(BF16)
        return 0

    lax.fori_loop(0, 8, scale_row, 0)

    @pl.when(has_up)
    def _():
        to_down.wait_recv()

    @pl.when(t == 0)
    def _():
        fx[0:3] = jnp.zeros((3, 192, 256), BF16)

    @pl.when(has_down)
    def _():
        to_up.wait_recv()

    @pl.when(t == 31)
    def _():
        fx[11:14] = jnp.zeros((3, 192, 256), BF16)

    def conv_halo(g, _):
        for r, slot in HALO_SLOTS:
            spread(fx[r, rows16(g), :], slot, g, xh)
        v = jnp.dot(taps_h[g], xh[g], preferred_element_type=F32)
        for i in (0, 1, 2, 5, 6, 7):
            zf[i, rows16(g), :] += v[i * 16 : i * 16 + 16, :]
        return 0

    lax.fori_loop(0, 12, conv_halo, 0)

    def norm(n, _):
        i = n // 2
        ln = pl.ds(pl.multiple_of(n % 2 * 128, 128), 128)
        v = zf[i, :, ln]
        v = v - jnp.sum(v, axis=0, keepdims=True) * (1.0 / 192)
        var = jnp.sum(v * v, axis=0, keepdims=True) * (1.0 / 192)
        r = lax.rsqrt(var + EPSILON)
        v = v * r
        zf[i, :, ln] = v
        rinv[i, :, ln] = jnp.broadcast_to(r, (8, 128))
        nb[i, :, ln] = (v * par[1, 0:192, :] + par[2, 0:192, :]).astype(BF16)
        return 0

    lax.fori_loop(0, 16, norm, 0)

    def stage0(f):
        pay[f] = gw[1 - core, f].astype(BF16)
        core_copy(f).start()

    def core_copy(f):
        return remote(pay.at[f], r0.at[f], ar_send.at[f, 0], ar_recv.at[f, 0], partner, t)

    def x_copies(f):
        return [
            remote(s1b.at[f, pl.ds(((x + d + 1) % 4) * 48, 48)], r1.at[f, d], ar_send.at[f, 1 + d], ar_recv.at[f, 1 + d], *x_peers[d])
            for d in range(3)
        ]

    def y_copies(f):
        return [remote(ry.at[f, y], ry.at[f, y], ar_send.at[f, 4 + d], ar_recv.at[f, 4 + d], *y_peers[d]) for d in range(3)]

    def z_copies(f):
        return [remote(rz.at[f, z], rz.at[f, z], ar_send.at[f, 7 + d], ar_recv.at[f, 7 + d], *z_peers[d]) for d in range(3)]

    def x_back(f):
        mine = full.at[core, f, pl.ds(x * 48, 48)]
        return [remote(mine, mine, ar_send.at[f, 10 + d], ar_recv.at[f, 10 + d], *x_peers[d]) for d in range(3)]

    def core_back(f):
        return remote(full.at[core, f], full.at[core, f], ar_send.at[f, 13], ar_recv.at[f, 13], partner, t)

    def stage1(f):
        core_copy(f).wait()
        total = gw[core, f] + r0[f].astype(F32)
        s1f[f] = total
        s1b[f] = total.astype(BF16)
        for c in x_copies(f):
            c.start()

    def stage2(f):
        for c in x_copies(f):
            c.wait()
        total = s1f[f, pl.ds(x * 48, 48), :]
        for d in range(3):
            total = total + r1[f, d].astype(F32)
        ry[f, y] = total
        for c in y_copies(f):
            c.start()

    def stage3(f):
        for c in y_copies(f):
            c.wait()
        rz[f, z] = (ry[f, 0] + ry[f, 1]) + (ry[f, 2] + ry[f, 3])
        for c in z_copies(f):
            c.start()

    def stage4(f):
        for c in z_copies(f):
            c.wait()
        full[core, f, pl.ds(x * 48, 48), :] = ((rz[f, 0] + rz[f, 1]) + (rz[f, 2] + rz[f, 3])).astype(BF16)
        for c in x_back(f):
            c.start()

    def stage5(f):
        for c in x_back(f):
            c.wait()
        core_back(f).start()

    def stage6(f):
        core_back(f).wait()
        out_gwi[:, f * 256 : f * 256 + 256] = full[0, f].astype(F32) * PIXEL_SCALE
        out_gwoT[:, f * 256 : f * 256 + 256] = full[1, f].astype(F32) * PIXEL_SCALE

    gw[...] = jnp.zeros_like(gw)
    osum[...] = jnp.zeros_like(osum)
    nsum[...] = jnp.zeros_like(nsum)
    after = {
        3: [(stage0, 0)], 4: [(stage1, 0)], 7: [(stage2, 0), (stage0, 1)], 8: [(stage1, 1)], 10: [(stage3, 0)],
        11: [(stage2, 1), (stage0, 2)],
    }

    def mlp(k, _):
        f = k // 4
        units = pl.ds(pl.multiple_of(f * 256, 256), 256)
        for m in range(2):
            i = k % 4 * 2 + m
            hidden = jnp.dot(winT[units, :], nb[i], preferred_element_type=F32) + both(bias[units, :])
            value, slope = gelu_parts(hidden)
            act = value.astype(BF16)
            gh = (jnp.dot(wout[units, :], gout[i], preferred_element_type=F32) * slope).astype(BF16)
            osum[i] += jnp.dot(woutT[:, units], act, preferred_element_type=F32)
            nsum[i] += jnp.dot(w_in[:, units], gh, preferred_element_type=F32)
            gw[0, f] += lax.dot_general(nb[i], gh, NT, preferred_element_type=F32)
            gw[1, f] += lax.dot_general(gout[i], act, NT, preferred_element_type=F32)
        for at, steps in after.items():

            @pl.when(k == at)
            def _():
                for step, chunk in steps:
                    step(chunk)

        return 0

    lax.fori_loop(0, 12, mlp, 0)

    def finish(n, _):
        i = n // 2
        ln = pl.ds(pl.multiple_of(n % 2 * 128, 128), 128)
        gn = nsum[i, :, ln] * par[1, 0:192, :]
        u = zf[i, :, ln]
        m1 = jnp.sum(gn, axis=0, keepdims=True) * (1.0 / 192)
        m2 = jnp.sum(gn * u, axis=0, keepdims=True) * (1.0 / 192)
        gzs[i, :, ln] = (rinv[i, 0:1, ln] * (gn - m1 - u * m2)).astype(BF16)
        branch = osum[i, :, ln] + par[3, 0:192, :]
        outs[i, :, ln] = (fx[i + 3, :, ln].astype(F32) + par[4, 0:192, :] * branch).astype(BF16)
        return 0

    lax.fori_loop(0, 16, finish, 0)

    gz_up = remote(gzs.at[pl.ds(0, 3)], halo.at[1], halo_send.at[2], halo_recv.at[2], s, up)
    gz_down = remote(gzs.at[pl.ds(5, 3)], halo.at[0], halo_send.at[3], halo_recv.at[3], s, down)

    @pl.when(has_up)
    def _():
        gz_up.start()

    @pl.when(has_down)
    def _():
        gz_down.start()

    block_out = pltpu.make_async_copy(outs, out_block.at[0, 0], out_sem.at[0])
    block_out.start()
    stage4(0)
    stage1(2)

    lane = lax.broadcasted_iota(jnp.int32, (8, 128), 1)
    sub = lax.broadcasted_iota(jnp.int32, (8, 128), 0)

    def taps_grad(g, _):
        for i in range(8):
            spread(gzs[i, rows16(g), :], i, g, gs)
        mine = gs[g, 3 * 128 : 3 * 128 + 128, :]
        for b in range(7):
            at_own = lax.dot_general(mine, xs[g, b * 128 : b * 128 + 128, :], NT, preferred_element_type=F32)
            at_halo = lax.dot_general(mine, xh[g, b * 128 : b * 128 + 128, :], NT, preferred_element_type=F32)
            total = jnp.zeros((8, 128), F32)
            for i in range(8):
                use_own, use_halo = valid(i, lane)
                v = jnp.zeros((8, 128), F32)
                for h in range(2):
                    at = i * 16 + h * 8
                    same = lane % 16 == sub + h * 8
                    v = jnp.where(same & use_own, at_own[at : at + 8], v)
                    if not 3 <= i < 5:
                        v = jnp.where(same & use_halo, at_halo[at : at + 8], v)
                total = total + (pltpu.roll(v, (3 - i) * 16 % 128, 1) if i != 3 else v)
            gkr[pl.ds(g * 8 + b, 1), :] = jnp.sum(total, axis=0, keepdims=True)
        return 0

    gkr[...] = jnp.zeros_like(gkr)
    lax.fori_loop(0, 6, taps_grad, 0)
    stage5(0)
    stage3(1)
    stage2(2)
    lax.fori_loop(6, 12, taps_grad, 0)

    other = pl.ds((1 - core) * 48, 48)
    own_half = pl.ds(core * 48, 48)
    k_core = remote(gkr.at[other], k0, k_send.at[0], k_recv.at[0], partner, t)
    k_core.start()
    stage6(0)

    def back_own(g, _):
        v = jnp.dot(back[g], gs[g], preferred_element_type=F32)
        for i in range(8):
            zf[i, rows16(g), :] = ct[i, rows16(g), :].astype(F32) + v[i * 16 : i * 16 + 16, :]
        return 0

    lax.fori_loop(0, 6, back_own, 0)
    k_core.wait()
    kx[x] = gkr[own_half, :] + k0[...]
    kx_copies = [remote(kx.at[x], kx.at[x], k_send.at[1 + d], k_recv.at[1 + d], *x_peers[d]) for d in range(3)]
    for c in kx_copies:
        c.start()
    stage4(1)
    stage3(2)
    lax.fori_loop(6, 12, back_own, 0)

    @pl.when(has_up)
    def _():
        gz_down.wait_recv()

    @pl.when(t == 0)
    def _():
        halo[0] = jnp.zeros((3, 192, 256), BF16)

    @pl.when(has_down)
    def _():
        gz_up.wait_recv()

    @pl.when(t == 31)
    def _():
        halo[1] = jnp.zeros((3, 192, 256), BF16)

    def back_halo(g, _):
        for r, slot in HALO_SLOTS:
            spread(halo[r // 8, r % 11, rows16(g), :], slot, g, gh_)
        v = jnp.dot(back_h[g], gh_[g], preferred_element_type=F32)
        for i in range(8):
            fx[i, rows16(g), :] = (zf[i, rows16(g), :] + v[i * 16 : i * 16 + 16, :]).astype(BF16)
        return 0

    for c in kx_copies:
        c.wait()
    ky[y] = (kx[0] + kx[1]) + (kx[2] + kx[3])
    ky_copies = [remote(ky.at[y], ky.at[y], k_send.at[4 + d], k_recv.at[4 + d], *y_peers[d]) for d in range(3)]
    for c in ky_copies:
        c.start()
    stage5(1)
    lax.fori_loop(0, 6, back_halo, 0)
    stage4(2)
    for c in ky_copies:
        c.wait()
    kz[z] = (ky[0] + ky[1]) + (ky[2] + ky[3])
    kz_copies = [remote(kz.at[z], kz.at[z], k_send.at[7 + d], k_recv.at[7 + d], *z_peers[d]) for d in range(3)]
    for c in kz_copies:
        c.start()
    stage6(1)
    lax.fori_loop(6, 12, back_halo, 0)
    gin_out = pltpu.make_async_copy(fx.at[pl.ds(0, 8)], out_gin.at[0, 0], out_sem.at[1])
    gin_out.start()
    stage5(2)
    for c in kz_copies:
        c.wait()
    kfull[own_half, :] = (kz[0] + kz[1]) + (kz[2] + kz[3])
    k_back = remote(kfull.at[own_half], kfull.at[own_half], k_send.at[10], k_recv.at[10], partner, t)
    k_back.start()
    stage6(2)
    k_back.wait()
    out_gk[...] = kfull[...] * PIXEL_SCALE

    @pl.when(has_up)
    def _():
        to_up.wait_send()
        gz_up.wait_send()

    @pl.when(has_down)
    def _():
        to_down.wait_send()
        gz_down.wait_send()

    block_out.wait()
    gin_out.wait()


def on_device(features, dw_kernel, dw_bias, ln_gain, ln_bias, w_in, b_in, w_out, b_out, layer_scale, cotangent):
    row = lambda v: v.reshape(1, -1)
    turn = lambda v: jnp.swapaxes(v, 3, 4)
    any_, vmem = pl.BlockSpec(memory_space=pl.ANY), pl.BlockSpec(memory_space=pltpu.VMEM)
    V, DMA = pltpu.VMEM, pltpu.SemaphoreType.DMA
    groups = V((12, 896, 256), BF16)
    tables = V((12, 128, 896), BF16)
    scratch = [
        V((14, 192, 256), BF16), V((8, 192, 256), BF16), groups, groups, groups, groups, tables, tables, tables, tables,
        V((19, 8, 256), F32), V((8, 192, 256), F32), V((5, 256, 128), F32), V((768, 128), F32), V((768, 192), BF16),
        V((768, 192), BF16), V((8, 192, 256), BF16),
        V((8, 192, 256), BF16), V((8, 8, 256), F32), V((8, 192, 256), F32), V((8, 192, 256), F32), V((8, 192, 256), BF16),
        V((8, 192, 256), BF16), V((2, 3, 192, 256), F32), V((96, 128), F32), V((2, 3, 192, 256), BF16),
        V((3, 192, 256), BF16), V((3, 192, 256), BF16), V((3, 192, 256), F32), V((3, 192, 256), BF16), V((3, 3, 48, 256), BF16),
        V((3, 4, 48, 256), F32), V((3, 4, 48, 256), F32), V((2, 3, 192, 256), BF16),
        V((48, 128), F32), V((4, 48, 128), F32), V((4, 48, 128), F32), V((4, 48, 128), F32), V((96, 128), F32),
        DMA((2,)), DMA((2,)), DMA((4,)), DMA((4,)), DMA((3, 14)), DMA((3, 14)), DMA((11,)), DMA((11,)),
    ]
    block, gin, gwi, gwoT, gk = pl.pallas_call(
        kernel,
        out_shape=(
            jax.ShapeDtypeStruct((1, 1, 8, 192, 256), BF16), jax.ShapeDtypeStruct((1, 1, 8, 192, 256), BF16),
            jax.ShapeDtypeStruct((192, 768), F32), jax.ShapeDtypeStruct((192, 768), F32), jax.ShapeDtypeStruct((96, 128), F32),
        ),
        in_specs=[any_, any_] + [vmem] * 9,
        out_specs=(any_, any_, vmem, vmem, vmem),
        scratch_shapes=scratch,
        compiler_params=pltpu.CompilerParams(collective_id=0, has_side_effects=True, vmem_limit_bytes=60 << 20),
    )(
        turn(features), turn(cotangent), dw_kernel, row(dw_bias), row(ln_gain), row(ln_bias), w_in, row(b_in), w_out.T, row(b_out),
        row(layer_scale),
    )
    gk = gk.reshape(12, 8, 8, 16)[:, :7, :7].transpose(2, 1, 0, 3).reshape(7, 7, 192)
    return turn(block), turn(gin), gwi, gwoT.T, gk


def solution(mesh):
    split, whole = P("slide", "space", None, None, None), P()
    return jax.shard_map(
        on_device,
        mesh=mesh,
        in_specs=(split,) + (whole,) * 9 + (split,),
        out_specs=(split, split, whole, whole, whole),
        check_vma=False,
    )
```

time: 123 us -> 85.7 us (0.70)
  Pallas kernels: 113 us -> 76.4 us
    pallas_call x1, Pallas kernels: 113 us -> 76.4 us  [on_device(): pl.pallas_call(kernel, out_shape=(jax.ShapeDtypeStruct((1, 1, 8, 192, 256...]
where the time goes in v2:
time: 85.7 us; the launch traced here: 85.3 us
  Pallas kernels  76.4 us (89%)
  local copies, waits for them, and re-layouts  8.17 us (10%)
    pallas_call x1, Pallas kernels, on_device(): pl.pallas_call(kernel, out_shape=(jax.ShapeDtypeStruct((1, 1, 8, 192, 256...  76.4 us
    unnamed x15, local copies, waits for them, and re-layouts  5.83 us
    reshape x2, local copies, waits for them, and re-layouts, on_device(): gk.reshape(12, 8, 8, 16)[:, :7, :7].transpose(2, 1, 0, 3).reshape(7, 7, 192)  1.74 us

profile of v2, /device:TPU:1, one launch (start us, length us, event | category | flops | bytes accessed | tf_op | source)
XLA Modules:
  0.0 85.3 jit_solution(11784885089594254216)
XLA Ops:
  0.6 0.0 copy-start.4
  0.6 0.7 copy-done.4
  1.3 0.6 reshape.37.b_in
  1.9 76.4 %shard_map.146 = (bf16[1,1,8,192,256]{4,3,2,1,0:T(8,128)(2,1)}, bf16[1,1,8,192,256]{4,3,2,1,0:T(8,128)(2,1)}, f32[192,768]{1,0:T(8,128)}, f32[192,768]{1,0:T(8,128)}, f32[96,128]{1,0:T(8,128)}) custom-call(bf16[1,1,8,192,256]{4,3,2,1,0:T(8,128)(2,1)} %bitcast.15, bf16[1,1,8,192,256]{4,3,2,1,0:T(8,128)(2,1)} %bitcast.16, f32[7,7,192]{2,1,0:T(8,128)} %dwk.1, ...), custom_call_target="tpu_custom_call" | custom-call | tf_op jit(solution)/shard_map/pallas_call | solution.py:498
  78.3 1.0 %reshape.40 = f32[12,8,8,16]{3,2,1,0:T(8,128)S(1)} reshape(f32[96,128]{1,0:T(8,128)} %get-tuple-element.14) | data formatting | bytes 98304 | tf_op jit(solution)/shard_map/reshape | solution.py:512
  79.3 0.0 copy-start.1
  79.3 0.1 copy.20
  79.4 0.8 reshape.41
  80.2 0.2 copy-done.1
  80.4 0.0 copy-start
  80.4 0.9 %copy.25 = bf16[1,1,8,256,192]{3,4,2,1,0:T(8,128)(2,1)} copy(bf16[1,1,8,256,192]{3,4,2,1,0:T(8,128)(2,1)S(1)} %bitcast.18) | data formatting | bytes 1572864
  81.3 0.5 copy-done
  81.8 0.0 copy-start.3
  81.8 0.9 %copy.26 = bf16[1,1,8,256,192]{3,4,2,1,0:T(8,128)(2,1)} copy(bf16[1,1,8,256,192]{3,4,2,1,0:T(8,128)(2,1)S(1)} %bitcast.17) | data formatting | bytes 1572864
  82.7 0.5 copy-done.3
  83.2 0.0 copy-start.2
  83.2 0.8 copy.27
  84.0 0.5 copy-done.2
  84.4 0.8 copy.28
  (1 shorter events, 0.0 us)
Async XLA Ops:
  0.6 0.7 copy-start.4
  79.3 1.1 %copy-start.1 = (bf16[1,1,8,192,256]{4,3,2,1,0:T(8,128)(2,1)S(1)}, bf16[1,1,8,192,256]{4,3,2,1,0:T(8,128)(2,1)}, u32[]{:S(2)}) copy-start(bf16[1,1,8,192,256]{4,3,2,1,0:T(8,128)(2,1)} %get-tuple-element.10) | copy-start | bytes 2359300
  80.4 1.4 %copy-start = (bf16[1,1,8,192,256]{4,3,2,1,0:T(8,128)(2,1)S(1)}, bf16[1,1,8,192,256]{4,3,2,1,0:T(8,128)(2,1)}, u32[]{:S(2)}) copy-start(bf16[1,1,8,192,256]{4,3,2,1,0:T(8,128)(2,1)} %get-tuple-element.11) | copy-start | bytes 2359300
  81.8 1.3 %copy-start.3 = (f32[192,768]{1,0:T(8,128)S(1)}, f32[192,768]{1,0:T(8,128)}, u32[]{:S(2)}) copy-start(f32[192,768]{1,0:T(8,128)} %get-tuple-element.22) | copy-start | bytes 1769476
  83.2 1.3 %copy-start.2 = (f32[192,768]{1,0:T(8,128)S(1)}, f32[192,768]{1,0:T(8,128)}, u32[]{:S(2)}) copy-start(f32[192,768]{1,0:T(8,128)} %get-tuple-element.13) | copy-start | bytes 1769476

commit v3 on v2

--- a/solution.py
+++ b/solution.py
@@ -21,9 +21,10 @@
 
 
 def gelu_parts(h):
-    cdf = 0.5 * (1.0 + lax.erf(h * 0.7071067811865476))
-    slope = cdf + h * jnp.exp(-0.5 * h * h) * 0.3989422804014327
-    return h * cdf, slope
+    r = h * 0.7071067811865476
+    cdf = 0.5 + 0.5 * lax.erf(r)
+    density = jnp.exp2(r * r * -1.4426950408889634)
+    return h * cdf, cdf + (h * 0.3989422804014327) * density
 
 
 def spread(value, slot, group, dst):
@@ -153,7 +154,7 @@
         par[n, 0:128, :] = jnp.broadcast_to(ref[:, 0:128], (128, 128)).T
         par[n, 128:256, :] = jnp.broadcast_to(both(ref[:, 128:192]), (128, 128)).T
     for n in range(6):
-        bias[n * 128 : n * 128 + 128, :] = jnp.broadcast_to(b_in[:, n * 128 : n * 128 + 128], (128, 128)).T
+        bias[n * 128 : n * 128 + 128, :] = jnp.broadcast_to(b_in[n * 128 : n * 128 + 128].reshape(1, 128), (128, 128)).T
     winT[...] = w_in[...].T
     wout[...] = woutT[...].T
     build_taps(dwk, flat, taps, taps_h, False)
@@ -177,7 +178,6 @@
         return 0
 
     lax.fori_loop(0, 12, conv_own, 0)
-    build_taps(dwk, flat, back, back_h, True)
     cot_in.wait()
 
     def scale_row(i, _):
@@ -185,32 +185,6 @@
         return 0
 
     lax.fori_loop(0, 8, scale_row, 0)
-
-    @pl.when(has_up)
-    def _():
-        to_down.wait_recv()
-
-    @pl.when(t == 0)
-    def _():
-        fx[0:3] = jnp.zeros((3, 192, 256), BF16)
-
-    @pl.when(has_down)
-    def _():
-        to_up.wait_recv()
-
-    @pl.when(t == 31)
-    def _():
-        fx[11:14] = jnp.zeros((3, 192, 256), BF16)
-
-    def conv_halo(g, _):
-        for r, slot in HALO_SLOTS:
-            spread(fx[r, rows16(g), :], slot, g, xh)
-        v = jnp.dot(taps_h[g], xh[g], preferred_element_type=F32)
-        for i in (0, 1, 2, 5, 6, 7):
-            zf[i, rows16(g), :] += v[i * 16 : i * 16 + 16, :]
-        return 0
-
-    lax.fori_loop(0, 12, conv_halo, 0)
 
     def norm(n, _):
         i = n // 2
@@ -225,7 +199,64 @@
         nb[i, :, ln] = (v * par[1, 0:192, :] + par[2, 0:192, :]).astype(BF16)
         return 0
 
-    lax.fori_loop(0, 16, norm, 0)
+    lax.fori_loop(6, 10, norm, 0)
+
+    gw[...] = jnp.zeros_like(gw)
+    osum[...] = jnp.zeros_like(osum)
+    nsum[...] = jnp.zeros_like(nsum)
+
+    def mlp_pair(f, p):
+        units = pl.ds(pl.multiple_of(f * 256, 256), 256)
+        q = 7 - p
+        normed = jnp.concatenate([nb[p], nb[q]], axis=1)
+        upper = jnp.concatenate([gout[p], gout[q]], axis=1)
+        hidden = jnp.dot(winT[units, :], normed, preferred_element_type=F32) + both(both(bias[units, :]))
+        value, slope = gelu_parts(hidden)
+        act = value.astype(BF16)
+        gh = (jnp.dot(wout[units, :], upper, preferred_element_type=F32) * slope).astype(BF16)
+        out = jnp.dot(woutT[:, units], act, preferred_element_type=F32)
+        osum[p] += out[:, 0:256]
+        osum[q] += out[:, 256:512]
+        out = jnp.dot(w_in[:, units], gh, preferred_element_type=F32)
+        nsum[p] += out[:, 0:256]
+        nsum[q] += out[:, 256:512]
+        gw[0, f] += lax.dot_general(normed, gh, NT, preferred_element_type=F32)
+        gw[1, f] += lax.dot_general(upper, act, NT, preferred_element_type=F32)
+
+    def mlp_inner(k, _):
+        mlp_pair(k, 3)
+        return 0
+
+    lax.fori_loop(0, 3, mlp_inner, 0)
+
+    @pl.when(has_up)
+    def _():
+        to_down.wait_recv()
+
+    @pl.when(t == 0)
+    def _():
+        fx[0:3] = jnp.zeros((3, 192, 256), BF16)
+
+    @pl.when(has_down)
+    def _():
+        to_up.wait_recv()
+
+    @pl.when(t == 31)
+    def _():
+        fx[11:14] = jnp.zeros((3, 192, 256), BF16)
+
+    def conv_halo(g, _):
+        for r, slot in HALO_SLOTS:
+            spread(fx[r, rows16(g), :], slot, g, xh)
+        v = jnp.dot(taps_h[g], xh[g], preferred_element_type=F32)
+        for i in (0, 1, 2, 5, 6, 7):
+            zf[i, rows16(g), :] += v[i * 16 : i * 16 + 16, :]
+        return 0
+
+    lax.fori_loop(0, 12, conv_halo, 0)
+
+    lax.fori_loop(0, 6, norm, 0)
+    lax.fori_loop(10, 16, norm, 0)
 
     def stage0(f):
         pay[f] = gw[1 - core, f].astype(BF16)
@@ -295,27 +326,12 @@
         out_gwi[:, f * 256 : f * 256 + 256] = full[0, f].astype(F32) * PIXEL_SCALE
         out_gwoT[:, f * 256 : f * 256 + 256] = full[1, f].astype(F32) * PIXEL_SCALE
 
-    gw[...] = jnp.zeros_like(gw)
-    osum[...] = jnp.zeros_like(osum)
-    nsum[...] = jnp.zeros_like(nsum)
     after = {
-        3: [(stage0, 0)], 4: [(stage1, 0)], 7: [(stage2, 0), (stage0, 1)], 8: [(stage1, 1)], 10: [(stage3, 0)],
-        11: [(stage2, 1), (stage0, 2)],
+        2: [(stage0, 0)], 4: [(stage1, 0)], 5: [(stage0, 1)], 7: [(stage2, 0), (stage1, 1)], 8: [(stage0, 2)],
     }
 
     def mlp(k, _):
-        f = k // 4
-        units = pl.ds(pl.multiple_of(f * 256, 256), 256)
-        for m in range(2):
-            i = k % 4 * 2 + m
-            hidden = jnp.dot(winT[units, :], nb[i], preferred_element_type=F32) + both(bias[units, :])
-            value, slope = gelu_parts(hidden)
-            act = value.astype(BF16)
-            gh = (jnp.dot(wout[units, :], gout[i], preferred_element_type=F32) * slope).astype(BF16)
-            osum[i] += jnp.dot(woutT[:, units], act, preferred_element_type=F32)
-            nsum[i] += jnp.dot(w_in[:, units], gh, preferred_element_type=F32)
-            gw[0, f] += lax.dot_general(nb[i], gh, NT, preferred_element_type=F32)
-            gw[1, f] += lax.dot_general(gout[i], act, NT, preferred_element_type=F32)
+        mlp_pair(k // 3, k % 3)
         for at, steps in after.items():
 
             @pl.when(k == at)
@@ -325,7 +341,7 @@
 
         return 0
 
-    lax.fori_loop(0, 12, mlp, 0)
+    lax.fori_loop(0, 9, mlp, 0)
 
     def finish(n, _):
         i = n // 2
@@ -335,6 +351,11 @@
         m1 = jnp.sum(gn, axis=0, keepdims=True) * (1.0 / 192)
         m2 = jnp.sum(gn * u, axis=0, keepdims=True) * (1.0 / 192)
         gzs[i, :, ln] = (rinv[i, 0:1, ln] * (gn - m1 - u * m2)).astype(BF16)
+        return 0
+
+    def finish_out(n, _):
+        i = n // 2
+        ln = pl.ds(pl.multiple_of(n % 2 * 128, 128), 128)
         branch = osum[i, :, ln] + par[3, 0:192, :]
         outs[i, :, ln] = (fx[i + 3, :, ln].astype(F32) + par[4, 0:192, :] * branch).astype(BF16)
         return 0
@@ -352,10 +373,9 @@
     def _():
         gz_down.start()
 
-    block_out = pltpu.make_async_copy(outs, out_block.at[0, 0], out_sem.at[0])
-    block_out.start()
-    stage4(0)
     stage1(2)
+    stage2(1)
+    stage3(0)
 
     lane = lax.broadcasted_iota(jnp.int32, (8, 128), 1)
     sub = lax.broadcasted_iota(jnp.int32, (8, 128), 0)
@@ -383,16 +403,21 @@
 
     gkr[...] = jnp.zeros_like(gkr)
     lax.fori_loop(0, 6, taps_grad, 0)
-    stage5(0)
+    stage2(2)
     stage3(1)
-    stage2(2)
+    stage4(0)
     lax.fori_loop(6, 12, taps_grad, 0)
 
     other = pl.ds((1 - core) * 48, 48)
     own_half = pl.ds(core * 48, 48)
     k_core = remote(gkr.at[other], k0, k_send.at[0], k_recv.at[0], partner, t)
     k_core.start()
-    stage6(0)
+    stage3(2)
+    stage4(1)
+    stage5(0)
+    lax.fori_loop(0, 16, finish_out, 0)
+    block_out = pltpu.make_async_copy(outs, out_block.at[0, 0], out_sem.at[0])
+    block_out.start()
 
     def back_own(g, _):
         v = jnp.dot(back[g], gs[g], preferred_element_type=F32)
@@ -400,40 +425,15 @@
             zf[i, rows16(g), :] = ct[i, rows16(g), :].astype(F32) + v[i * 16 : i * 16 + 16, :]
         return 0
 
-    lax.fori_loop(0, 6, back_own, 0)
     k_core.wait()
     kx[x] = gkr[own_half, :] + k0[...]
     kx_copies = [remote(kx.at[x], kx.at[x], k_send.at[1 + d], k_recv.at[1 + d], *x_peers[d]) for d in range(3)]
     for c in kx_copies:
         c.start()
-    stage4(1)
-    stage3(2)
-    lax.fori_loop(6, 12, back_own, 0)
-
-    @pl.when(has_up)
-    def _():
-        gz_down.wait_recv()
-
-    @pl.when(t == 0)
-    def _():
-        halo[0] = jnp.zeros((3, 192, 256), BF16)
-
-    @pl.when(has_down)
-    def _():
-        gz_up.wait_recv()
-
-    @pl.when(t == 31)
-    def _():
-        halo[1] = jnp.zeros((3, 192, 256), BF16)
-
-    def back_halo(g, _):
-        for r, slot in HALO_SLOTS:
-            spread(halo[r // 8, r % 11, rows16(g), :], slot, g, gh_)
-        v = jnp.dot(back_h[g], gh_[g], preferred_element_type=F32)
-        for i in range(8):
-            fx[i, rows16(g), :] = (zf[i, rows16(g), :] + v[i * 16 : i * 16 + 16, :]).astype(BF16)
-        return 0
-
+    build_taps(dwk, flat, back, back_h, True)
+    stage4(2)
+    stage6(0)
+    lax.fori_loop(0, 12, back_own, 0)
     for c in kx_copies:
         c.wait()
     ky[y] = (kx[0] + kx[1]) + (kx[2] + kx[3])
@@ -441,8 +441,7 @@
     for c in ky_copies:
         c.start()
     stage5(1)
-    lax.fori_loop(0, 6, back_halo, 0)
-    stage4(2)
+    stage5(2)
     for c in ky_copies:
         c.wait()
     kz[z] = (ky[0] + ky[1]) + (ky[2] + ky[3])
@@ -450,18 +449,50 @@
     for c in kz_copies:
         c.start()
     stage6(1)
-    lax.fori_loop(6, 12, back_halo, 0)
-    gin_out = pltpu.make_async_copy(fx.at[pl.ds(0, 8)], out_gin.at[0, 0], out_sem.at[1])
-    gin_out.start()
-    stage5(2)
+    stage6(2)
+
+    @pl.when(has_up)
+    def _():
+        gz_down.wait_recv()
+
+    @pl.when(t == 0)
+    def _():
+        halo[0] = jnp.zeros((3, 192, 256), BF16)
+
+    @pl.when(has_down)
+    def _():
+        gz_up.wait_recv()
+
+    @pl.when(t == 31)
+    def _():
+        halo[1] = jnp.zeros((3, 192, 256), BF16)
+
+    def back_halo(g, _):
+        for r, slot in HALO_SLOTS:
+            spread(halo[r // 8, r % 11, rows16(g), :], slot, g, gh_)
+        v = jnp.dot(back_h[g], gh_[g], preferred_element_type=F32)
+        for i in range(8):
+            fx[i, rows16(g), :] = (zf[i, rows16(g), :] + v[i * 16 : i * 16 + 16, :]).astype(BF16)
+        return 0
+
+    lax.fori_loop(0, 6, back_halo, 0)
     for c in kz_copies:
         c.wait()
     kfull[own_half, :] = (kz[0] + kz[1]) + (kz[2] + kz[3])
     k_back = remote(kfull.at[own_half], kfull.at[own_half], k_send.at[10], k_recv.at[10], partner, t)
     k_back.start()
-    stage6(2)
+    lax.fori_loop(6, 12, back_halo, 0)
+    gin_out = pltpu.make_async_copy(fx.at[pl.ds(0, 8)], out_gin.at[0, 0], out_sem.at[1])
+    gin_out.start()
     k_back.wait()
-    out_gk[...] = kfull[...] * PIXEL_SCALE
+    for a in range(7):
+        for tile, width in ((0, 128), (128, 64)):
+            base = jnp.zeros((8, 128), F32)
+            for g in range(tile // 16, (tile + width) // 16):
+                at = g % 8 * 16
+                v = pltpu.roll(kfull[g * 8 : g * 8 + 8, :], (at - a * 16) % 128, 1)
+                base = jnp.where((lane >= at) & (lane < at + 16), v, base)
+            out_gk[a, :, tile : tile + width] = base[0:7, 0:width] * PIXEL_SCALE
 
     @pl.when(has_up)
     def _():
@@ -475,6 +506,30 @@
 
     block_out.wait()
     gin_out.wait()
+
+
+def hand_over_kernel(*refs):
+    ins, outs, held, sems = refs[:5], refs[5:10], refs[10:15], refs[15]
+    loads = [pltpu.make_async_copy(i, h, sems.at[0, n]) for n, (i, h) in enumerate(zip(ins, held))]
+    stores = [pltpu.make_async_copy(h, o, sems.at[1, n]) for n, (h, o) in enumerate(zip(held, outs))]
+    for c in loads:
+        c.start()
+    for load, store in zip(loads, stores):
+        load.wait()
+        store.start()
+    for c in stores:
+        c.wait()
+
+
+def hand_over(*values):
+    shapes = tuple(jax.ShapeDtypeStruct(v.shape, v.dtype) for v in values)
+    return pl.pallas_call(
+        hand_over_kernel,
+        out_shape=shapes,
+        in_specs=[pl.BlockSpec(memory_space=pl.ANY)] * 5,
+        out_specs=(pl.BlockSpec(memory_space=pl.ANY),) * 5,
+        scratch_shapes=[pltpu.VMEM(v.shape, v.dtype) for v in values] + [pltpu.SemaphoreType.DMA((2, 5))],
+    )(*values)
 
 
 def on_device(features, dw_kernel, dw_bias, ln_gain, ln_bias, w_in, b_in, w_out, b_out, layer_scale, cotangent):
@@ -499,17 +554,17 @@
         kernel,
         out_shape=(
             jax.ShapeDtypeStruct((1, 1, 8, 192, 256), BF16), jax.ShapeDtypeStruct((1, 1, 8, 192, 256), BF16),
-            jax.ShapeDtypeStruct((192, 768), F32), jax.ShapeDtypeStruct((192, 768), F32), jax.ShapeDtypeStruct((96, 128), F32),
+            jax.ShapeDtypeStruct((192, 768), F32), jax.ShapeDtypeStruct((192, 768), F32), jax.ShapeDtypeStruct((7, 7, 192), F32),
         ),
         in_specs=[any_, any_] + [vmem] * 9,
         out_specs=(any_, any_, vmem, vmem, vmem),
         scratch_shapes=scratch,
         compiler_params=pltpu.CompilerParams(collective_id=0, has_side_effects=True, vmem_limit_bytes=60 << 20),
     )(
-        turn(features), turn(cotangent), dw_kernel, row(dw_bias), row(ln_gain), row(ln_bias), w_in, row(b_in), w_out.T, row(b_out),
+        turn(features), turn(cotangent), dw_kernel, row(dw_bias), row(ln_gain), row(ln_bias), w_in, b_in, w_out.T, row(b_out),
         row(layer_scale),
     )
-    gk = gk.reshape(12, 8, 8, 16)[:, :7, :7].transpose(2, 1, 0, 3).reshape(7, 7, 192)
+    block, gin, gwi, gwoT, gk = hand_over(block, gin, gwi, gwoT, gk)
     return turn(block), turn(gin), gwi, gwoT.T, gk
 
 

time: 85.7 us -> 81.1 us (0.946)
  local copies, waits for them, and re-layouts: 8.17 us -> 0 us
  Pallas kernels: 76.4 us -> 79.5 us
    unnamed x15 -> x0, local copies, waits for them, and re-layouts: 5.83 us -> none
    pallas_call x0 -> x1, Pallas kernels: none -> 2.75 us  [hand_over(): pl.pallas_call(hand_over_kernel, out_shape=shapes, in_specs=[pl.BlockSpec...]
    reshape x3 -> x0, local copies, waits for them, and re-layouts: 2.32 us -> none  [the longest x2 1.74 us: on_device(): gk.reshape(12, 8, 8, 16)[:, :7, :7].transpose(2, 1, 0, 3).reshape(7, 7, 192)]
where the time goes in v3:
time: 81.1 us; the launch traced here: 80.2 us
  Pallas kernels  79.5 us (98%)
    pallas_call x1, Pallas kernels, on_device(): pl.pallas_call(kernel, out_shape=(jax.ShapeDtypeStruct((1, 1, 8, 192, 256...  76.8 us
    pallas_call x1, Pallas kernels, hand_over(): pl.pallas_call(hand_over_kernel, out_shape=shapes, in_specs=[pl.BlockSpec...  2.75 us

profile of v3, /device:TPU:1, one launch (start us, length us, event | category | flops | bytes accessed | tf_op | source)
XLA Modules:
  0.0 80.2 jit_solution(6428020791873438234)
XLA Ops:
  0.6 76.8 %shard_map.146 = (bf16[1,1,8,192,256]{4,3,2,1,0:T(8,128)(2,1)}, bf16[1,1,8,192,256]{4,3,2,1,0:T(8,128)(2,1)}, f32[192,768]{1,0:T(8,128)}, f32[192,768]{1,0:T(8,128)}, f32[7,7,192]{2,1,0:T(8,128)}) custom-call(bf16[1,1,8,192,256]{4,3,2,1,0:T(8,128)(2,1)} %bitcast.11, bf16[1,1,8,192,256]{4,3,2,1,0:T(8,128)(2,1)} %bitcast.12, f32[7,7,192]{2,1,0:T(8,128)} %dwk.1, ...), custom_call_target="tpu_custom_call" | custom-call | tf_op jit(solution)/shard_map/pallas_call | solution.py:553
  77.4 2.8 %shard_map.147 = (bf16[1,1,8,192,256]{4,3,2,1,0:T(8,128)(2,1)}, bf16[1,1,8,192,256]{4,3,2,1,0:T(8,128)(2,1)}, f32[192,768]{1,0:T(8,128)}, f32[192,768]{1,0:T(8,128)}, f32[7,7,192]{2,1,0:T(8,128)}) custom-call(bf16[1,1,8,192,256]{4,3,2,1,0:T(8,128)(2,1)} %get-tuple-element.15.refs_0_, bf16[1,1,8,192,256]{4,3,2,1,0:T(8,128)(2,1)} %get-tuple-element.16.refs_1_, ...), custom_call_target="tpu_custom_call" | custom-call | tf_op jit(solution)/shard_map/pallas_call | solution.py:526

commit v4 on v3

--- a/solution.py
+++ b/solution.py
@@ -106,7 +106,7 @@
     out_block, out_gin, out_gwi, out_gwoT, out_gk,
     fx, ct, xs, xh, gs, gh_, taps, taps_h, back, back_h, flat, zf, par, bias, winT, wout, gout,
     nb, rinv, osum, nsum, outs, gzs, gw, gkr, halo,
-    pay, r0, s1f, s1b, r1, ry, rz, full, k0, kx, ky, kz, kfull,
+    pay, r0, s1f, s1b, r1, s2, r2, rz, fa, full, k0, kx, ky, kz, kfull,
     in_sem, out_sem, halo_send, halo_recv, ar_send, ar_recv, k_send, k_recv,
 ):
     s, t = lax.axis_index("slide"), lax.axis_index("space")
@@ -265,63 +265,78 @@
     def core_copy(f):
         return remote(pay.at[f], r0.at[f], ar_send.at[f, 0], ar_recv.at[f, 0], partner, t)
 
+    def y_copies(f):
+        return [
+            remote(s1b.at[f, pl.ds(((y + d + 1) % 4) * 48, 48)], r1.at[f, d], ar_send.at[f, 1 + d], ar_recv.at[f, 1 + d], *y_peers[d])
+            for d in range(3)
+        ]
+
     def x_copies(f):
         return [
-            remote(s1b.at[f, pl.ds(((x + d + 1) % 4) * 48, 48)], r1.at[f, d], ar_send.at[f, 1 + d], ar_recv.at[f, 1 + d], *x_peers[d])
-            for d in range(3)
+            remote(s2.at[f, (x + d + 1) % 4], r2.at[f, d], ar_send.at[f, 4 + d], ar_recv.at[f, 4 + d], *x_peers[d]) for d in range(3)
         ]
-
-    def y_copies(f):
-        return [remote(ry.at[f, y], ry.at[f, y], ar_send.at[f, 4 + d], ar_recv.at[f, 4 + d], *y_peers[d]) for d in range(3)]
 
     def z_copies(f):
         return [remote(rz.at[f, z], rz.at[f, z], ar_send.at[f, 7 + d], ar_recv.at[f, 7 + d], *z_peers[d]) for d in range(3)]
 
     def x_back(f):
-        mine = full.at[core, f, pl.ds(x * 48, 48)]
-        return [remote(mine, mine, ar_send.at[f, 10 + d], ar_recv.at[f, 10 + d], *x_peers[d]) for d in range(3)]
+        return [remote(fa.at[f, x], fa.at[f, x], ar_send.at[f, 10 + d], ar_recv.at[f, 10 + d], *x_peers[d]) for d in range(3)]
+
+    def y_back(f):
+        mine = full.at[core, f, pl.ds(y * 48, 48)]
+        return [remote(mine, mine, ar_send.at[f, 13 + d], ar_recv.at[f, 13 + d], *y_peers[d]) for d in range(3)]
 
     def core_back(f):
-        return remote(full.at[core, f], full.at[core, f], ar_send.at[f, 13], ar_recv.at[f, 13], partner, t)
+        return remote(full.at[core, f], full.at[core, f], ar_send.at[f, 16], ar_recv.at[f, 16], partner, t)
 
     def stage1(f):
         core_copy(f).wait()
         total = gw[core, f] + r0[f].astype(F32)
         s1f[f] = total
         s1b[f] = total.astype(BF16)
+        for c in y_copies(f):
+            c.start()
+
+    def stage2(f):
+        for c in y_copies(f):
+            c.wait()
+        total = s1f[f, pl.ds(y * 48, 48), :]
+        for d in range(3):
+            total = total + r1[f, d].astype(F32)
+        for part in range(4):
+            at, ln = part % 2 * 24, part // 2 * 128
+            s2[f, part] = total[at : at + 24, ln : ln + 128]
         for c in x_copies(f):
             c.start()
 
-    def stage2(f):
+    def stage3(f):
         for c in x_copies(f):
             c.wait()
-        total = s1f[f, pl.ds(x * 48, 48), :]
-        for d in range(3):
-            total = total + r1[f, d].astype(F32)
-        ry[f, y] = total
-        for c in y_copies(f):
-            c.start()
-
-    def stage3(f):
-        for c in y_copies(f):
-            c.wait()
-        rz[f, z] = (ry[f, 0] + ry[f, 1]) + (ry[f, 2] + ry[f, 3])
+        rz[f, z] = (s2[f, x] + r2[f, 0]) + (r2[f, 1] + r2[f, 2])
         for c in z_copies(f):
             c.start()
 
     def stage4(f):
         for c in z_copies(f):
             c.wait()
-        full[core, f, pl.ds(x * 48, 48), :] = ((rz[f, 0] + rz[f, 1]) + (rz[f, 2] + rz[f, 3])).astype(BF16)
+        fa[f, x] = (rz[f, 0] + rz[f, 1]) + (rz[f, 2] + rz[f, 3])
         for c in x_back(f):
             c.start()
 
     def stage5(f):
         for c in x_back(f):
             c.wait()
+        rows = [jnp.concatenate([fa[f, part], fa[f, part + 2]], axis=1) for part in range(2)]
+        full[core, f, pl.ds(pl.multiple_of(y * 48, 16), 48), :] = jnp.concatenate(rows, axis=0).astype(BF16)
+        for c in y_back(f):
+            c.start()
+
+    def stage6(f):
+        for c in y_back(f):
+            c.wait()
         core_back(f).start()
 
-    def stage6(f):
+    def stage7(f):
         core_back(f).wait()
         out_gwi[:, f * 256 : f * 256 + 256] = full[0, f].astype(F32) * PIXEL_SCALE
         out_gwoT[:, f * 256 : f * 256 + 256] = full[1, f].astype(F32) * PIXEL_SCALE
@@ -362,17 +377,19 @@
 
     lax.fori_loop(0, 16, finish, 0)
 
-    gz_up = remote(gzs.at[pl.ds(0, 3)], halo.at[1], halo_send.at[2], halo_recv.at[2], s, up)
-    gz_down = remote(gzs.at[pl.ds(5, 3)], halo.at[0], halo_send.at[3], halo_recv.at[3], s, down)
-
-    @pl.when(has_up)
-    def _():
-        gz_up.start()
-
-    @pl.when(has_down)
-    def _():
-        gz_down.start()
-
+    gz_up = [remote(gzs.at[n], halo.at[1, n], halo_send.at[2 + n], halo_recv.at[2 + n], s, up) for n in range(3)]
+    gz_down = [remote(gzs.at[7 - n], halo.at[0, 2 - n], halo_send.at[5 + n], halo_recv.at[5 + n], s, down) for n in range(3)]
+
+    def send_row(n):
+        @pl.when(has_up)
+        def _():
+            gz_up[n].start()
+
+        @pl.when(has_down)
+        def _():
+            gz_down[n].start()
+
+    send_row(0)
     stage1(2)
     stage2(1)
     stage3(0)
@@ -402,19 +419,31 @@
         return 0
 
     gkr[...] = jnp.zeros_like(gkr)
-    lax.fori_loop(0, 6, taps_grad, 0)
-    stage2(2)
-    stage3(1)
-    stage4(0)
-    lax.fori_loop(6, 12, taps_grad, 0)
+    def taps_step(g, _):
+        taps_grad(g, 0)
+
+        @pl.when(g == 3)
+        def _():
+            send_row(1)
+            stage2(2)
+            stage3(1)
+            stage4(0)
+
+        @pl.when(g == 8)
+        def _():
+            send_row(2)
+            stage3(2)
+            stage4(1)
+            stage5(0)
+
+        return 0
+
+    lax.fori_loop(0, 12, taps_step, 0)
 
     other = pl.ds((1 - core) * 48, 48)
     own_half = pl.ds(core * 48, 48)
     k_core = remote(gkr.at[other], k0, k_send.at[0], k_recv.at[0], partner, t)
     k_core.start()
-    stage3(2)
-    stage4(1)
-    stage5(0)
     lax.fori_loop(0, 16, finish_out, 0)
     block_out = pltpu.make_async_copy(outs, out_block.at[0, 0], out_sem.at[0])
     block_out.start()
@@ -426,34 +455,38 @@
         return 0
 
     k_core.wait()
-    kx[x] = gkr[own_half, :] + k0[...]
-    kx_copies = [remote(kx.at[x], kx.at[x], k_send.at[1 + d], k_recv.at[1 + d], *x_peers[d]) for d in range(3)]
+    ky[y] = gkr[own_half, :] + k0[...]
+    ky_copies = [remote(ky.at[y], ky.at[y], k_send.at[1 + d], k_recv.at[1 + d], *y_peers[d]) for d in range(3)]
+    for c in ky_copies:
+        c.start()
+    stage4(2)
+    stage5(1)
+    stage6(0)
+    build_taps(dwk, flat, back, back_h, True)
+    for c in ky_copies:
+        c.wait()
+    kx[x] = (ky[0] + ky[1]) + (ky[2] + ky[3])
+    kx_copies = [remote(kx.at[x], kx.at[x], k_send.at[4 + d], k_recv.at[4 + d], *x_peers[d]) for d in range(3)]
     for c in kx_copies:
         c.start()
-    build_taps(dwk, flat, back, back_h, True)
-    stage4(2)
-    stage6(0)
+    stage5(2)
+    stage6(1)
+    stage7(0)
     lax.fori_loop(0, 12, back_own, 0)
     for c in kx_copies:
         c.wait()
-    ky[y] = (kx[0] + kx[1]) + (kx[2] + kx[3])
-    ky_copies = [remote(ky.at[y], ky.at[y], k_send.at[4 + d], k_recv.at[4 + d], *y_peers[d]) for d in range(3)]
-    for c in ky_copies:
-        c.start()
-    stage5(1)
-    stage5(2)
-    for c in ky_copies:
-        c.wait()
-    kz[z] = (ky[0] + ky[1]) + (ky[2] + ky[3])
+    kz[z] = (kx[0] + kx[1]) + (kx[2] + kx[3])
     kz_copies = [remote(kz.at[z], kz.at[z], k_send.at[7 + d], k_recv.at[7 + d], *z_peers[d]) for d in range(3)]
     for c in kz_copies:
         c.start()
-    stage6(1)
     stage6(2)
+    stage7(1)
+    stage7(2)
 
     @pl.when(has_up)
     def _():
-        gz_down.wait_recv()
+        for c in gz_down:
+            c.wait_recv()
 
     @pl.when(t == 0)
     def _():
@@ -461,7 +494,8 @@
 
     @pl.when(has_down)
     def _():
-        gz_up.wait_recv()
+        for c in gz_up:
+            c.wait_recv()
 
     @pl.when(t == 31)
     def _():
@@ -497,12 +531,14 @@
     @pl.when(has_up)
     def _():
         to_up.wait_send()
-        gz_up.wait_send()
+        for c in gz_up:
+            c.wait_send()
 
     @pl.when(has_down)
     def _():
         to_down.wait_send()
-        gz_down.wait_send()
+        for c in gz_down:
+            c.wait_send()
 
     block_out.wait()
     gin_out.wait()
@@ -546,9 +582,9 @@
         V((8, 192, 256), BF16), V((8, 8, 256), F32), V((8, 192, 256), F32), V((8, 192, 256), F32), V((8, 192, 256), BF16),
         V((8, 192, 256), BF16), V((2, 3, 192, 256), F32), V((96, 128), F32), V((2, 3, 192, 256), BF16),
         V((3, 192, 256), BF16), V((3, 192, 256), BF16), V((3, 192, 256), F32), V((3, 192, 256), BF16), V((3, 3, 48, 256), BF16),
-        V((3, 4, 48, 256), F32), V((3, 4, 48, 256), F32), V((2, 3, 192, 256), BF16),
+        V((3, 4, 24, 128), F32), V((3, 3, 24, 128), F32), V((3, 4, 24, 128), F32), V((3, 4, 24, 128), F32), V((2, 3, 192, 256), BF16),
         V((48, 128), F32), V((4, 48, 128), F32), V((4, 48, 128), F32), V((4, 48, 128), F32), V((96, 128), F32),
-        DMA((2,)), DMA((2,)), DMA((4,)), DMA((4,)), DMA((3, 14)), DMA((3, 14)), DMA((11,)), DMA((11,)),
+        DMA((2,)), DMA((2,)), DMA((8,)), DMA((8,)), DMA((3, 17)), DMA((3, 17)), DMA((11,)), DMA((11,)),
     ]
     block, gin, gwi, gwoT, gk = pl.pallas_call(
         kernel,

time: 81.1 us -> 75.2 us (0.927)
  Pallas kernels: 79.5 us -> 74.4 us
    pallas_call x1, Pallas kernels: 76.8 us -> 71.6 us  [on_device(): pl.pallas_call(kernel, out_shape=(jax.ShapeDtypeStruct((1, 1, 8, 192, 256...]
where the time goes in v4:
time: 75.2 us; the launch traced here: 75 us
  Pallas kernels  74.4 us (99%)
    pallas_call x1, Pallas kernels, on_device(): pl.pallas_call(kernel, out_shape=(jax.ShapeDtypeStruct((1, 1, 8, 192, 256...  71.6 us
    pallas_call x1, Pallas kernels, hand_over(): pl.pallas_call(hand_over_kernel, out_shape=shapes, in_specs=[pl.BlockSpec...  2.75 us

profile of v4, /device:TPU:1, one launch (start us, length us, event | category | flops | bytes accessed | tf_op | source)
XLA Modules:
  0.0 75.0 jit_solution(2560053175790064860)
XLA Ops:
  0.6 71.6 %shard_map.146 = (bf16[1,1,8,192,256]{4,3,2,1,0:T(8,128)(2,1)}, bf16[1,1,8,192,256]{4,3,2,1,0:T(8,128)(2,1)}, f32[192,768]{1,0:T(8,128)}, f32[192,768]{1,0:T(8,128)}, f32[7,7,192]{2,1,0:T(8,128)}) custom-call(bf16[1,1,8,192,256]{4,3,2,1,0:T(8,128)(2,1)} %bitcast.11, bf16[1,1,8,192,256]{4,3,2,1,0:T(8,128)(2,1)} %bitcast.12, f32[7,7,192]{2,1,0:T(8,128)} %dwk.1, ...), custom_call_target="tpu_custom_call" | custom-call | tf_op jit(solution)/shard_map/pallas_call | solution.py:589
  72.3 2.8 %shard_map.147 = (bf16[1,1,8,192,256]{4,3,2,1,0:T(8,128)(2,1)}, bf16[1,1,8,192,256]{4,3,2,1,0:T(8,128)(2,1)}, f32[192,768]{1,0:T(8,128)}, f32[192,768]{1,0:T(8,128)}, f32[7,7,192]{2,1,0:T(8,128)}) custom-call(bf16[1,1,8,192,256]{4,3,2,1,0:T(8,128)(2,1)} %get-tuple-element.15.refs_0_, bf16[1,1,8,192,256]{4,3,2,1,0:T(8,128)(2,1)} %get-tuple-element.16.refs_1_, ...), custom_call_target="tpu_custom_call" | custom-call | tf_op jit(solution)/shard_map/pallas_call | solution.py:562

commit v5 on v4

--- a/solution.py
+++ b/solution.py
@@ -103,7 +103,7 @@
 
 def kernel(
     feat, cot, dwk, dwb, gain, lbias, w_in, b_in, woutT, b_out, lscale,
-    out_block, out_gin, out_gwi, out_gwoT, out_gk,
+    out_block, out_gin, out_full, out_gk,
     fx, ct, xs, xh, gs, gh_, taps, taps_h, back, back_h, flat, zf, par, bias, winT, wout, gout,
     nb, rinv, osum, nsum, outs, gzs, gw, gkr, halo,
     pay, r0, s1f, s1b, r1, s2, r2, rz, fa, full, k0, kx, ky, kz, kfull,
@@ -283,11 +283,11 @@
         return [remote(fa.at[f, x], fa.at[f, x], ar_send.at[f, 10 + d], ar_recv.at[f, 10 + d], *x_peers[d]) for d in range(3)]
 
     def y_back(f):
-        mine = full.at[core, f, pl.ds(y * 48, 48)]
+        mine = full.at[f, core, pl.ds(y * 48, 48)]
         return [remote(mine, mine, ar_send.at[f, 13 + d], ar_recv.at[f, 13 + d], *y_peers[d]) for d in range(3)]
 
     def core_back(f):
-        return remote(full.at[core, f], full.at[core, f], ar_send.at[f, 16], ar_recv.at[f, 16], partner, t)
+        return remote(full.at[f, core], full.at[f, core], ar_send.at[f, 16], ar_recv.at[f, 16], partner, t)
 
     def stage1(f):
         core_copy(f).wait()
@@ -327,7 +327,7 @@
         for c in x_back(f):
             c.wait()
         rows = [jnp.concatenate([fa[f, part], fa[f, part + 2]], axis=1) for part in range(2)]
-        full[core, f, pl.ds(pl.multiple_of(y * 48, 16), 48), :] = jnp.concatenate(rows, axis=0).astype(BF16)
+        full[f, core, pl.ds(pl.multiple_of(y * 48, 16), 48), :] = jnp.concatenate(rows, axis=0).astype(BF16)
         for c in y_back(f):
             c.start()
 
@@ -338,8 +338,10 @@
 
     def stage7(f):
         core_back(f).wait()
-        out_gwi[:, f * 256 : f * 256 + 256] = full[0, f].astype(F32) * PIXEL_SCALE
-        out_gwoT[:, f * 256 : f * 256 + 256] = full[1, f].astype(F32) * PIXEL_SCALE
+        full_out(f).start()
+
+    def full_out(f):
+        return pltpu.make_async_copy(full.at[f], out_full.at[f], out_sem.at[2 + f])
 
     after = {
         2: [(stage0, 0)], 4: [(stage1, 0)], 5: [(stage0, 1)], 7: [(stage2, 0), (stage1, 1)], 8: [(stage0, 2)],
@@ -389,8 +391,8 @@
         def _():
             gz_down[n].start()
 
+    stage1(2)
     send_row(0)
-    stage1(2)
     stage2(1)
     stage3(0)
 
@@ -398,12 +400,11 @@
     sub = lax.broadcasted_iota(jnp.int32, (8, 128), 0)
 
     def taps_grad(g, _):
-        for i in range(8):
-            spread(gzs[i, rows16(g), :], i, g, gs)
-        mine = gs[g, 3 * 128 : 3 * 128 + 128, :]
+        mine = jnp.concatenate([gzs[i, rows16(g), :] for i in range(8)], axis=0)
         for b in range(7):
-            at_own = lax.dot_general(mine, xs[g, b * 128 : b * 128 + 128, :], NT, preferred_element_type=F32)
-            at_halo = lax.dot_general(mine, xh[g, b * 128 : b * 128 + 128, :], NT, preferred_element_type=F32)
+            rows = pl.ds(b * 128, 128)
+            pairs = lax.dot_general(mine, jnp.concatenate([xs[g, rows, :], xh[g, rows, :]], axis=0), NT, preferred_element_type=F32)
+            at_own, at_halo = pairs[:, 0:128], pairs[:, 128:256]
             total = jnp.zeros((8, 128), F32)
             for i in range(8):
                 use_own, use_halo = valid(i, lane)
@@ -422,19 +423,12 @@
     def taps_step(g, _):
         taps_grad(g, 0)
 
-        @pl.when(g == 3)
+        @pl.when(g == 5)
         def _():
+            stage2(2)
             send_row(1)
-            stage2(2)
             stage3(1)
             stage4(0)
-
-        @pl.when(g == 8)
-        def _():
-            send_row(2)
-            stage3(2)
-            stage4(1)
-            stage5(0)
 
         return 0
 
@@ -444,11 +438,17 @@
     own_half = pl.ds(core * 48, 48)
     k_core = remote(gkr.at[other], k0, k_send.at[0], k_recv.at[0], partner, t)
     k_core.start()
+    stage3(2)
+    send_row(2)
+    stage4(1)
+    stage5(0)
     lax.fori_loop(0, 16, finish_out, 0)
     block_out = pltpu.make_async_copy(outs, out_block.at[0, 0], out_sem.at[0])
     block_out.start()
 
     def back_own(g, _):
+        for i in range(8):
+            spread(gzs[i, rows16(g), :], i, g, gs)
         v = jnp.dot(back[g], gs[g], preferred_element_type=F32)
         for i in range(8):
             zf[i, rows16(g), :] = ct[i, rows16(g), :].astype(F32) + v[i * 16 : i * 16 + 16, :]
@@ -459,10 +459,11 @@
     ky_copies = [remote(ky.at[y], ky.at[y], k_send.at[1 + d], k_recv.at[1 + d], *y_peers[d]) for d in range(3)]
     for c in ky_copies:
         c.start()
+    build_taps(dwk, flat, back, back_h, True)
     stage4(2)
     stage5(1)
     stage6(0)
-    build_taps(dwk, flat, back, back_h, True)
+    lax.fori_loop(0, 4, back_own, 0)
     for c in ky_copies:
         c.wait()
     kx[x] = (ky[0] + ky[1]) + (ky[2] + ky[3])
@@ -471,8 +472,7 @@
         c.start()
     stage5(2)
     stage6(1)
-    stage7(0)
-    lax.fori_loop(0, 12, back_own, 0)
+    lax.fori_loop(4, 12, back_own, 0)
     for c in kx_copies:
         c.wait()
     kz[z] = (kx[0] + kx[1]) + (kx[2] + kx[3])
@@ -480,8 +480,8 @@
     for c in kz_copies:
         c.start()
     stage6(2)
+    stage7(0)
     stage7(1)
-    stage7(2)
 
     @pl.when(has_up)
     def _():
@@ -509,15 +509,23 @@
             fx[i, rows16(g), :] = (zf[i, rows16(g), :] + v[i * 16 : i * 16 + 16, :]).astype(BF16)
         return 0
 
-    lax.fori_loop(0, 6, back_halo, 0)
-    for c in kz_copies:
-        c.wait()
-    kfull[own_half, :] = (kz[0] + kz[1]) + (kz[2] + kz[3])
+    def back_step(g, _):
+        back_halo(g, 0)
+
+        @pl.when(g == 5)
+        def _():
+            for c in kz_copies:
+                c.wait()
+            kfull[own_half, :] = (kz[0] + kz[1]) + (kz[2] + kz[3])
+            k_back.start()
+
+        return 0
+
     k_back = remote(kfull.at[own_half], kfull.at[own_half], k_send.at[10], k_recv.at[10], partner, t)
-    k_back.start()
-    lax.fori_loop(6, 12, back_halo, 0)
+    lax.fori_loop(0, 12, back_step, 0)
     gin_out = pltpu.make_async_copy(fx.at[pl.ds(0, 8)], out_gin.at[0, 0], out_sem.at[1])
     gin_out.start()
+    stage7(2)
     k_back.wait()
     for a in range(7):
         for tile, width in ((0, 128), (128, 64)):
@@ -542,30 +550,45 @@
 
     block_out.wait()
     gin_out.wait()
-
-
-def hand_over_kernel(*refs):
-    ins, outs, held, sems = refs[:5], refs[5:10], refs[10:15], refs[15]
-    loads = [pltpu.make_async_copy(i, h, sems.at[0, n]) for n, (i, h) in enumerate(zip(ins, held))]
-    stores = [pltpu.make_async_copy(h, o, sems.at[1, n]) for n, (h, o) in enumerate(zip(held, outs))]
+    for f in range(3):
+        full_out(f).wait()
+
+
+def hand_over_kernel(
+    block, gin, full, gk, out_block, out_gin, out_gk, out_gwi, out_gwoT, h_block, h_gin, h_gk, h_full, h_gwi, h_gwoT, sems
+):
+    plain = ((block, h_block, out_block), (gin, h_gin, out_gin), (gk, h_gk, out_gk))
+    load = pltpu.make_async_copy(full, h_full, sems.at[0, 3])
+    load.start()
+    loads = [pltpu.make_async_copy(i, h, sems.at[0, n]) for n, (i, h, o) in enumerate(plain)]
+    stores = [pltpu.make_async_copy(h, o, sems.at[1, n]) for n, (i, h, o) in enumerate(plain)]
     for c in loads:
         c.start()
-    for load, store in zip(loads, stores):
-        load.wait()
+    load.wait()
+    for m, (held, out) in enumerate(((h_gwi, out_gwi), (h_gwoT, out_gwoT))):
+        for f in range(3):
+            held[:, f * 256 : f * 256 + 256] = h_full[f, m].astype(F32) * PIXEL_SCALE
+        stores.append(pltpu.make_async_copy(held, out, sems.at[1, 3 + m]))
+        stores[-1].start()
+    for c, store in zip(loads, stores):
+        c.wait()
         store.start()
     for c in stores:
         c.wait()
 
 
-def hand_over(*values):
-    shapes = tuple(jax.ShapeDtypeStruct(v.shape, v.dtype) for v in values)
+def hand_over(block, gin, full, gk):
+    like = lambda v: jax.ShapeDtypeStruct(v.shape, v.dtype)
+    weights = jax.ShapeDtypeStruct((192, 768), F32)
+    shapes = (like(block), like(gin), like(gk), weights, weights)
     return pl.pallas_call(
         hand_over_kernel,
         out_shape=shapes,
-        in_specs=[pl.BlockSpec(memory_space=pl.ANY)] * 5,
+        in_specs=[pl.BlockSpec(memory_space=pl.ANY)] * 4,
         out_specs=(pl.BlockSpec(memory_space=pl.ANY),) * 5,
-        scratch_shapes=[pltpu.VMEM(v.shape, v.dtype) for v in values] + [pltpu.SemaphoreType.DMA((2, 5))],
-    )(*values)
+        scratch_shapes=[pltpu.VMEM(v.shape, v.dtype) for v in (block, gin, gk, full, weights, weights)]
+        + [pltpu.SemaphoreType.DMA((2, 5))],
+    )(block, gin, full, gk)
 
 
 def on_device(features, dw_kernel, dw_bias, ln_gain, ln_bias, w_in, b_in, w_out, b_out, layer_scale, cotangent):
@@ -582,25 +605,25 @@
         V((8, 192, 256), BF16), V((8, 8, 256), F32), V((8, 192, 256), F32), V((8, 192, 256), F32), V((8, 192, 256), BF16),
         V((8, 192, 256), BF16), V((2, 3, 192, 256), F32), V((96, 128), F32), V((2, 3, 192, 256), BF16),
         V((3, 192, 256), BF16), V((3, 192, 256), BF16), V((3, 192, 256), F32), V((3, 192, 256), BF16), V((3, 3, 48, 256), BF16),
-        V((3, 4, 24, 128), F32), V((3, 3, 24, 128), F32), V((3, 4, 24, 128), F32), V((3, 4, 24, 128), F32), V((2, 3, 192, 256), BF16),
+        V((3, 4, 24, 128), F32), V((3, 3, 24, 128), F32), V((3, 4, 24, 128), F32), V((3, 4, 24, 128), F32), V((3, 2, 192, 256), BF16),
         V((48, 128), F32), V((4, 48, 128), F32), V((4, 48, 128), F32), V((4, 48, 128), F32), V((96, 128), F32),
-        DMA((2,)), DMA((2,)), DMA((8,)), DMA((8,)), DMA((3, 17)), DMA((3, 17)), DMA((11,)), DMA((11,)),
+        DMA((2,)), DMA((5,)), DMA((8,)), DMA((8,)), DMA((3, 17)), DMA((3, 17)), DMA((11,)), DMA((11,)),
     ]
-    block, gin, gwi, gwoT, gk = pl.pallas_call(
+    values = pl.pallas_call(
         kernel,
         out_shape=(
             jax.ShapeDtypeStruct((1, 1, 8, 192, 256), BF16), jax.ShapeDtypeStruct((1, 1, 8, 192, 256), BF16),
-            jax.ShapeDtypeStruct((192, 768), F32), jax.ShapeDtypeStruct((192, 768), F32), jax.ShapeDtypeStruct((7, 7, 192), F32),
+            jax.ShapeDtypeStruct((3, 2, 192, 256), BF16), jax.ShapeDtypeStruct((7, 7, 192), F32),
         ),
         in_specs=[any_, any_] + [vmem] * 9,
-        out_specs=(any_, any_, vmem, vmem, vmem),
+        out_specs=(any_, any_, any_, vmem),
         scratch_shapes=scratch,
         compiler_params=pltpu.CompilerParams(collective_id=0, has_side_effects=True, vmem_limit_bytes=60 << 20),
     )(
         turn(features), turn(cotangent), dw_kernel, row(dw_bias), row(ln_gain), row(ln_bias), w_in, b_in, w_out.T, row(b_out),
         row(layer_scale),
     )
-    block, gin, gwi, gwoT, gk = hand_over(block, gin, gwi, gwoT, gk)
+    block, gin, gk, gwi, gwoT = hand_over(*values)
     return turn(block), turn(gin), gwi, gwoT.T, gk
 
 

time: 75.2 us -> 74.6 us (level); the launches traced: 75 us -> 73.6 us
  Pallas kernels: 74.4 us -> 72.9 us
    pallas_call x1, Pallas kernels: 71.6 us -> 70.2 us  [on_device(): pl.pallas_call(kernel, out_shape=(jax.ShapeDtypeStruct((1, 1, 8, 192, 256...]
where the time goes in v5:
time: 74.6 us; the launch traced here: 73.6 us
  Pallas kernels  72.9 us (98%)
    pallas_call x1, Pallas kernels, on_device(): pl.pallas_call(kernel, out_shape=(jax.ShapeDtypeStruct((1, 1, 8, 192, 256...  70.2 us
    pallas_call x1, Pallas kernels, hand_over(): pl.pallas_call(hand_over_kernel, out_shape=shapes, in_specs=[pl.BlockSpec...  2.72 us

profile of v5, /device:TPU:1, one launch (start us, length us, event | category | flops | bytes accessed | tf_op | source)
XLA Modules:
  0.0 73.6 jit_solution(8469441176290217097)
XLA Ops:
  0.6 70.2 %shard_map.146 = (bf16[1,1,8,192,256]{4,3,2,1,0:T(8,128)(2,1)}, bf16[1,1,8,192,256]{4,3,2,1,0:T(8,128)(2,1)}, bf16[3,2,192,256]{3,2,1,0:T(8,128)(2,1)}, f32[7,7,192]{2,1,0:T(8,128)}) custom-call(bf16[1,1,8,192,256]{4,3,2,1,0:T(8,128)(2,1)} %bitcast.11, bf16[1,1,8,192,256]{4,3,2,1,0:T(8,128)(2,1)} %bitcast.12, f32[7,7,192]{2,1,0:T(8,128)} %dwk.1, ...), custom_call_target="tpu_custom_call" | custom-call | tf_op jit(solution)/shard_map/pallas_call | solution.py:612
  70.9 2.7 %shard_map.147 = (bf16[1,1,8,192,256]{4,3,2,1,0:T(8,128)(2,1)}, bf16[1,1,8,192,256]{4,3,2,1,0:T(8,128)(2,1)}, f32[7,7,192]{2,1,0:T(8,128)}, f32[192,768]{1,0:T(8,128)}, f32[192,768]{1,0:T(8,128)}) custom-call(bf16[1,1,8,192,256]{4,3,2,1,0:T(8,128)(2,1)} %get-tuple-element.14.block, bf16[1,1,8,192,256]{4,3,2,1,0:T(8,128)(2,1)} %get-tuple-element.15.gin, ...), custom_call_target="tpu_custom_call" | custom-call | tf_op jit(solution)/shard_map/pallas_call | solution.py:584

commit v6 on v5

--- a/solution.py
+++ b/solution.py
@@ -106,17 +106,23 @@
     out_block, out_gin, out_full, out_gk,
     fx, ct, xs, xh, gs, gh_, taps, taps_h, back, back_h, flat, zf, par, bias, winT, wout, gout,
     nb, rinv, osum, nsum, outs, gzs, gw, gkr, halo,
-    pay, r0, s1f, s1b, r1, s2, r2, rz, fa, full, k0, kx, ky, kz, kfull,
-    in_sem, out_sem, halo_send, halo_recv, ar_send, ar_recv, k_send, k_recv,
+    pa, ra, rb, fc, rk, rk2, fk,
+    in_sem, out_sem, halo_send, halo_recv, ar_send, ar_recv,
 ):
     s, t = lax.axis_index("slide"), lax.axis_index("space")
     z_hi, core = s // 2, s % 2
-    z_lo, x, y = t % 2, (t // 2) % 4, t // 8
+    z_lo = t % 2
     z = z_hi * 2 + z_lo
-    partner = z_hi * 2 + (1 - core)
-    x_peers = [(s, (y * 4 + (x + d) % 4) * 2 + z_lo) for d in (1, 2, 3)]
-    y_peers = [(s, (((y + d) % 4) * 4 + x) * 2 + z_lo) for d in (1, 2, 3)]
-    z_peers = [(((z + d) % 4) // 2 * 2 + core, (y * 4 + x) * 2 + ((z + d) % 4) % 2) for d in (1, 2, 3)]
+    plane, pillar = t // 2, z * 2 + core
+    plane_peers = [((plane + e) % 16) for e in range(1, 16)]
+    pillar_peers = [((pillar + e) % 8) for e in range(1, 8)]
+
+    def in_plane(p):
+        return s, p * 2 + z_lo
+
+    def in_pillar(q):
+        return q // 4 * 2 + q % 2, plane * 2 + q // 2 % 2
+
     has_up, has_down = t > 0, t < 31
     up, down = jnp.maximum(t - 1, 0), jnp.minimum(t + 1, 31)
 
@@ -126,7 +132,7 @@
     cot_in.start()
 
     barrier = pltpu.get_barrier_semaphore()
-    for ps, pt in [(partner, t)] + x_peers + y_peers + z_peers:
+    for ps, pt in [in_plane(p) for p in plane_peers] + [in_pillar(q) for q in pillar_peers]:
         pl.semaphore_signal(barrier, inc=1, device_id={"slide": ps, "space": pt}, device_id_type=MESH)
 
     @pl.when(has_up)
@@ -137,7 +143,7 @@
     def _():
         pl.semaphore_signal(barrier, inc=1, device_id={"slide": s, "space": down}, device_id_type=MESH)
 
-    pl.semaphore_wait(barrier, 10 + jnp.minimum(t, 1) + jnp.minimum(31 - t, 1))
+    pl.semaphore_wait(barrier, 22 + jnp.minimum(t, 1) + jnp.minimum(31 - t, 1))
 
     to_up = remote(feat.at[0, 0, pl.ds(0, 3)], fx.at[pl.ds(11, 3)], halo_send.at[0], halo_recv.at[0], s, up)
     to_down = remote(feat.at[0, 0, pl.ds(5, 3)], fx.at[pl.ds(0, 3)], halo_send.at[1], halo_recv.at[1], s, down)
@@ -258,94 +264,66 @@
     lax.fori_loop(0, 6, norm, 0)
     lax.fori_loop(10, 16, norm, 0)
 
-    def stage0(f):
-        pay[f] = gw[1 - core, f].astype(BF16)
-        core_copy(f).start()
-
-    def core_copy(f):
-        return remote(pay.at[f], r0.at[f], ar_send.at[f, 0], ar_recv.at[f, 0], partner, t)
-
-    def y_copies(f):
+    def buffers(f):
+        return (gkr, rk, rk2, fk) if f == 3 else (pa.at[f], ra.at[f], rb.at[f], fc.at[f])
+
+    def spread_copies(f):
+        own, got, _, _ = buffers(f)
         return [
-            remote(s1b.at[f, pl.ds(((y + d + 1) % 4) * 48, 48)], r1.at[f, d], ar_send.at[f, 1 + d], ar_recv.at[f, 1 + d], *y_peers[d])
-            for d in range(3)
+            remote(own.at[p], got.at[e], ar_send.at[f, e], ar_recv.at[f, e], *in_plane(p)) for e, p in enumerate(plane_peers)
         ]
 
-    def x_copies(f):
+    def pillar_copies(f):
+        part = buffers(f)[2].at[pillar]
         return [
-            remote(s2.at[f, (x + d + 1) % 4], r2.at[f, d], ar_send.at[f, 4 + d], ar_recv.at[f, 4 + d], *x_peers[d]) for d in range(3)
+            remote(part, part, ar_send.at[f, 15 + e], ar_recv.at[f, 15 + e], *in_pillar(q)) for e, q in enumerate(pillar_peers)
         ]
 
-    def z_copies(f):
-        return [remote(rz.at[f, z], rz.at[f, z], ar_send.at[f, 7 + d], ar_recv.at[f, 7 + d], *z_peers[d]) for d in range(3)]
-
-    def x_back(f):
-        return [remote(fa.at[f, x], fa.at[f, x], ar_send.at[f, 10 + d], ar_recv.at[f, 10 + d], *x_peers[d]) for d in range(3)]
-
-    def y_back(f):
-        mine = full.at[f, core, pl.ds(y * 48, 48)]
-        return [remote(mine, mine, ar_send.at[f, 13 + d], ar_recv.at[f, 13 + d], *y_peers[d]) for d in range(3)]
-
-    def core_back(f):
-        return remote(full.at[f, core], full.at[f, core], ar_send.at[f, 16], ar_recv.at[f, 16], partner, t)
-
-    def stage1(f):
-        core_copy(f).wait()
-        total = gw[core, f] + r0[f].astype(F32)
-        s1f[f] = total
-        s1b[f] = total.astype(BF16)
-        for c in y_copies(f):
+    def back_copies(f):
+        part = buffers(f)[3].at[plane]
+        return [
+            remote(part, part, ar_send.at[f, 22 + e], ar_recv.at[f, 22 + e], *in_plane(p)) for e, p in enumerate(plane_peers)
+        ]
+
+    def full_out(f):
+        return pltpu.make_async_copy(fc.at[f], out_full.at[f], out_sem.at[2 + f])
+
+    def stage_a(f):
+        if f < 3:
+            for j in range(16):
+                at, ln = j % 8 * 24, j // 8 * 128
+                part = [gw[m, f, at : at + 24, ln : ln + 128] for m in range(2)]
+                pa[f, j] = jnp.concatenate(part, axis=0).astype(BF16)
+        for c in spread_copies(f):
             c.start()
 
-    def stage2(f):
-        for c in y_copies(f):
+    def stage_b(f):
+        for c in spread_copies(f):
             c.wait()
-        total = s1f[f, pl.ds(y * 48, 48), :]
-        for d in range(3):
-            total = total + r1[f, d].astype(F32)
-        for part in range(4):
-            at, ln = part % 2 * 24, part // 2 * 128
-            s2[f, part] = total[at : at + 24, ln : ln + 128]
-        for c in x_copies(f):
+        own, got, mine, _ = buffers(f)
+        total = own[plane].astype(F32)
+        for e in range(15):
+            total = total + got[e].astype(F32)
+        mine[pillar] = total
+        for c in pillar_copies(f):
             c.start()
 
-    def stage3(f):
-        for c in x_copies(f):
+    def stage_c(f):
+        for c in pillar_copies(f):
             c.wait()
-        rz[f, z] = (s2[f, x] + r2[f, 0]) + (r2[f, 1] + r2[f, 2])
-        for c in z_copies(f):
+        _, _, mine, result = buffers(f)
+        total = ((mine[0] + mine[1]) + (mine[2] + mine[3])) + ((mine[4] + mine[5]) + (mine[6] + mine[7]))
+        result[plane] = total.astype(result.dtype)
+        for c in back_copies(f):
             c.start()
 
-    def stage4(f):
-        for c in z_copies(f):
+    def stage_d(f):
+        for c in back_copies(f):
             c.wait()
-        fa[f, x] = (rz[f, 0] + rz[f, 1]) + (rz[f, 2] + rz[f, 3])
-        for c in x_back(f):
-            c.start()
-
-    def stage5(f):
-        for c in x_back(f):
-            c.wait()
-        rows = [jnp.concatenate([fa[f, part], fa[f, part + 2]], axis=1) for part in range(2)]
-        full[f, core, pl.ds(pl.multiple_of(y * 48, 16), 48), :] = jnp.concatenate(rows, axis=0).astype(BF16)
-        for c in y_back(f):
-            c.start()
-
-    def stage6(f):
-        for c in y_back(f):
-            c.wait()
-        core_back(f).start()
-
-    def stage7(f):
-        core_back(f).wait()
-        full_out(f).start()
-
-    def full_out(f):
-        return pltpu.make_async_copy(full.at[f], out_full.at[f], out_sem.at[2 + f])
-
-    after = {
-        2: [(stage0, 0)], 4: [(stage1, 0)], 5: [(stage0, 1)], 7: [(stage2, 0), (stage1, 1)], 8: [(stage0, 2)],
-    }
+        if f < 3:
+            full_out(f).start()
+
+    after = {2: [(stage_a, 0)], 5: [(stage_a, 1)], 8: [(stage_a, 2), (stage_b, 0)]}
 
     def mlp(k, _):
         mlp_pair(k // 3, k % 3)
@@ -391,10 +369,7 @@
         def _():
             gz_down[n].start()
 
-    stage1(2)
     send_row(0)
-    stage2(1)
-    stage3(0)
 
     lane = lax.broadcasted_iota(jnp.int32, (8, 128), 1)
     sub = lax.broadcasted_iota(jnp.int32, (8, 128), 0)
@@ -416,7 +391,7 @@
                     if not 3 <= i < 5:
                         v = jnp.where(same & use_halo, at_halo[at : at + 8], v)
                 total = total + (pltpu.roll(v, (3 - i) * 16 % 128, 1) if i != 3 else v)
-            gkr[pl.ds(g * 8 + b, 1), :] = jnp.sum(total, axis=0, keepdims=True)
+            gkr[g, b : b + 1, :] = jnp.sum(total, axis=0, keepdims=True)
         return 0
 
     gkr[...] = jnp.zeros_like(gkr)
@@ -425,26 +400,23 @@
 
         @pl.when(g == 5)
         def _():
-            stage2(2)
             send_row(1)
-            stage3(1)
-            stage4(0)
+            stage_b(1)
+            stage_c(0)
 
         return 0
 
     lax.fori_loop(0, 12, taps_step, 0)
 
-    other = pl.ds((1 - core) * 48, 48)
-    own_half = pl.ds(core * 48, 48)
-    k_core = remote(gkr.at[other], k0, k_send.at[0], k_recv.at[0], partner, t)
-    k_core.start()
-    stage3(2)
+    stage_a(3)
+    stage_b(2)
     send_row(2)
-    stage4(1)
-    stage5(0)
     lax.fori_loop(0, 16, finish_out, 0)
     block_out = pltpu.make_async_copy(outs, out_block.at[0, 0], out_sem.at[0])
     block_out.start()
+    stage_c(1)
+    stage_d(0)
+    build_taps(dwk, flat, back, back_h, True)
 
     def back_own(g, _):
         for i in range(8):
@@ -454,34 +426,18 @@
             zf[i, rows16(g), :] = ct[i, rows16(g), :].astype(F32) + v[i * 16 : i * 16 + 16, :]
         return 0
 
-    k_core.wait()
-    ky[y] = gkr[own_half, :] + k0[...]
-    ky_copies = [remote(ky.at[y], ky.at[y], k_send.at[1 + d], k_recv.at[1 + d], *y_peers[d]) for d in range(3)]
-    for c in ky_copies:
-        c.start()
-    build_taps(dwk, flat, back, back_h, True)
-    stage4(2)
-    stage5(1)
-    stage6(0)
-    lax.fori_loop(0, 4, back_own, 0)
-    for c in ky_copies:
-        c.wait()
-    kx[x] = (ky[0] + ky[1]) + (ky[2] + ky[3])
-    kx_copies = [remote(kx.at[x], kx.at[x], k_send.at[4 + d], k_recv.at[4 + d], *x_peers[d]) for d in range(3)]
-    for c in kx_copies:
-        c.start()
-    stage5(2)
-    stage6(1)
-    lax.fori_loop(4, 12, back_own, 0)
-    for c in kx_copies:
-        c.wait()
-    kz[z] = (kx[0] + kx[1]) + (kx[2] + kx[3])
-    kz_copies = [remote(kz.at[z], kz.at[z], k_send.at[7 + d], k_recv.at[7 + d], *z_peers[d]) for d in range(3)]
-    for c in kz_copies:
-        c.start()
-    stage6(2)
-    stage7(0)
-    stage7(1)
+    def back_own_step(g, _):
+        back_own(g, 0)
+
+        @pl.when(g == 4)
+        def _():
+            stage_c(2)
+
+        return 0
+
+    lax.fori_loop(0, 12, back_own_step, 0)
+    stage_b(3)
+    stage_d(1)
 
     @pl.when(has_up)
     def _():
@@ -514,25 +470,21 @@
 
         @pl.when(g == 5)
         def _():
-            for c in kz_copies:
-                c.wait()
-            kfull[own_half, :] = (kz[0] + kz[1]) + (kz[2] + kz[3])
-            k_back.start()
-
-        return 0
-
-    k_back = remote(kfull.at[own_half], kfull.at[own_half], k_send.at[10], k_recv.at[10], partner, t)
+            stage_c(3)
+
+        return 0
+
     lax.fori_loop(0, 12, back_step, 0)
     gin_out = pltpu.make_async_copy(fx.at[pl.ds(0, 8)], out_gin.at[0, 0], out_sem.at[1])
     gin_out.start()
-    stage7(2)
-    k_back.wait()
+    stage_d(2)
+    stage_d(3)
     for a in range(7):
         for tile, width in ((0, 128), (128, 64)):
             base = jnp.zeros((8, 128), F32)
             for g in range(tile // 16, (tile + width) // 16):
                 at = g % 8 * 16
-                v = pltpu.roll(kfull[g * 8 : g * 8 + 8, :], (at - a * 16) % 128, 1)
+                v = pltpu.roll(fk[g], (at - a * 16) % 128, 1)
                 base = jnp.where((lane >= at) & (lane < at + 16), v, base)
             out_gk[a, :, tile : tile + width] = base[0:7, 0:width] * PIXEL_SCALE
 
@@ -565,9 +517,13 @@
     for c in loads:
         c.start()
     load.wait()
+    for f in range(3):
+        for j in range(16):
+            part = h_full[f, j].astype(F32) * PIXEL_SCALE
+            at, ln = j % 8 * 24, f * 256 + j // 8 * 128
+            h_gwi[at : at + 24, ln : ln + 128] = part[0:24]
+            h_gwoT[at : at + 24, ln : ln + 128] = part[24:48]
     for m, (held, out) in enumerate(((h_gwi, out_gwi), (h_gwoT, out_gwoT))):
-        for f in range(3):
-            held[:, f * 256 : f * 256 + 256] = h_full[f, m].astype(F32) * PIXEL_SCALE
         stores.append(pltpu.make_async_copy(held, out, sems.at[1, 3 + m]))
         stores[-1].start()
     for c, store in zip(loads, stores):
@@ -603,17 +559,16 @@
         V((19, 8, 256), F32), V((8, 192, 256), F32), V((5, 256, 128), F32), V((768, 128), F32), V((768, 192), BF16),
         V((768, 192), BF16), V((8, 192, 256), BF16),
         V((8, 192, 256), BF16), V((8, 8, 256), F32), V((8, 192, 256), F32), V((8, 192, 256), F32), V((8, 192, 256), BF16),
-        V((8, 192, 256), BF16), V((2, 3, 192, 256), F32), V((96, 128), F32), V((2, 3, 192, 256), BF16),
-        V((3, 192, 256), BF16), V((3, 192, 256), BF16), V((3, 192, 256), F32), V((3, 192, 256), BF16), V((3, 3, 48, 256), BF16),
-        V((3, 4, 24, 128), F32), V((3, 3, 24, 128), F32), V((3, 4, 24, 128), F32), V((3, 4, 24, 128), F32), V((3, 2, 192, 256), BF16),
-        V((48, 128), F32), V((4, 48, 128), F32), V((4, 48, 128), F32), V((4, 48, 128), F32), V((96, 128), F32),
-        DMA((2,)), DMA((5,)), DMA((8,)), DMA((8,)), DMA((3, 17)), DMA((3, 17)), DMA((11,)), DMA((11,)),
+        V((8, 192, 256), BF16), V((2, 3, 192, 256), F32), V((16, 8, 128), F32), V((2, 3, 192, 256), BF16),
+        V((3, 16, 48, 128), BF16), V((3, 15, 48, 128), BF16), V((3, 8, 48, 128), F32), V((3, 16, 48, 128), BF16),
+        V((15, 8, 128), F32), V((8, 8, 128), F32), V((16, 8, 128), F32),
+        DMA((2,)), DMA((5,)), DMA((8,)), DMA((8,)), DMA((4, 37)), DMA((4, 37)),
     ]
     values = pl.pallas_call(
         kernel,
         out_shape=(
             jax.ShapeDtypeStruct((1, 1, 8, 192, 256), BF16), jax.ShapeDtypeStruct((1, 1, 8, 192, 256), BF16),
-            jax.ShapeDtypeStruct((3, 2, 192, 256), BF16), jax.ShapeDtypeStruct((7, 7, 192), F32),
+            jax.ShapeDtypeStruct((3, 16, 48, 128), BF16), jax.ShapeDtypeStruct((7, 7, 192), F32),
         ),
         in_specs=[any_, any_] + [vmem] * 9,
         out_specs=(any_, any_, any_, vmem),

time: 74.6 us -> 76.4 us (1.024); the launches traced: 73.6 us -> 76.3 us
  Pallas kernels: 72.9 us -> 75.6 us
    pallas_call x1, Pallas kernels: 70.2 us -> 72.9 us  [on_device(): pl.pallas_call(kernel, out_shape=(jax.ShapeDtypeStruct((1, 1, 8, 192, 256...]
where the time goes in v6:
time: 76.4 us; the launch traced here: 76.3 us
  Pallas kernels  75.6 us (99%)
    pallas_call x1, Pallas kernels, on_device(): pl.pallas_call(kernel, out_shape=(jax.ShapeDtypeStruct((1, 1, 8, 192, 256...  72.9 us
    pallas_call x1, Pallas kernels, hand_over(): pl.pallas_call(hand_over_kernel, out_shape=shapes, in_specs=[pl.BlockSpec...  2.72 us

profile of v6, /device:TPU:1, one launch (start us, length us, event | category | flops | bytes accessed | tf_op | source)
XLA Modules:
  0.0 76.3 jit_solution(17365693376506611973)
XLA Ops:
  0.6 72.9 %shard_map.146 = (bf16[1,1,8,192,256]{4,3,2,1,0:T(8,128)(2,1)}, bf16[1,1,8,192,256]{4,3,2,1,0:T(8,128)(2,1)}, bf16[3,16,48,128]{3,2,1,0:T(8,128)(2,1)}, f32[7,7,192]{2,1,0:T(8,128)}) custom-call(bf16[1,1,8,192,256]{4,3,2,1,0:T(8,128)(2,1)} %bitcast.11, bf16[1,1,8,192,256]{4,3,2,1,0:T(8,128)(2,1)} %bitcast.12, f32[7,7,192]{2,1,0:T(8,128)} %dwk.1, ...), custom_call_target="tpu_custom_call" | custom-call | tf_op jit(solution)/shard_map/pallas_call | solution.py:567
  73.5 2.7 %shard_map.147 = (bf16[1,1,8,192,256]{4,3,2,1,0:T(8,128)(2,1)}, bf16[1,1,8,192,256]{4,3,2,1,0:T(8,128)(2,1)}, f32[7,7,192]{2,1,0:T(8,128)}, f32[192,768]{1,0:T(8,128)}, f32[192,768]{1,0:T(8,128)}) custom-call(bf16[1,1,8,192,256]{4,3,2,1,0:T(8,128)(2,1)} %get-tuple-element.14.block, bf16[1,1,8,192,256]{4,3,2,1,0:T(8,128)(2,1)} %get-tuple-element.15.gin, ...), custom_call_target="tpu_custom_call" | custom-call | tf_op jit(solution)/shard_map/pallas_call | solution.py:540

commit v7 on v6

--- a/solution.py
+++ b/solution.py
@@ -304,7 +304,7 @@
         total = own[plane].astype(F32)
         for e in range(15):
             total = total + got[e].astype(F32)
-        mine[pillar] = total
+        mine[pillar] = total.astype(mine.dtype)
         for c in pillar_copies(f):
             c.start()
 
@@ -312,7 +312,9 @@
         for c in pillar_copies(f):
             c.wait()
         _, _, mine, result = buffers(f)
-        total = ((mine[0] + mine[1]) + (mine[2] + mine[3])) + ((mine[4] + mine[5]) + (mine[6] + mine[7]))
+        total = mine[0].astype(F32)
+        for q in range(1, 8):
+            total = total + mine[q].astype(F32)
         result[plane] = total.astype(result.dtype)
         for c in back_copies(f):
             c.start()
@@ -322,21 +324,6 @@
             c.wait()
         if f < 3:
             full_out(f).start()
-
-    after = {2: [(stage_a, 0)], 5: [(stage_a, 1)], 8: [(stage_a, 2), (stage_b, 0)]}
-
-    def mlp(k, _):
-        mlp_pair(k // 3, k % 3)
-        for at, steps in after.items():
-
-            @pl.when(k == at)
-            def _():
-                for step, chunk in steps:
-                    step(chunk)
-
-        return 0
-
-    lax.fori_loop(0, 9, mlp, 0)
 
     def finish(n, _):
         i = n // 2
@@ -355,8 +342,6 @@
         outs[i, :, ln] = (fx[i + 3, :, ln].astype(F32) + par[4, 0:192, :] * branch).astype(BF16)
         return 0
 
-    lax.fori_loop(0, 16, finish, 0)
-
     gz_up = [remote(gzs.at[n], halo.at[1, n], halo_send.at[2 + n], halo_recv.at[2 + n], s, up) for n in range(3)]
     gz_down = [remote(gzs.at[7 - n], halo.at[0, 2 - n], halo_send.at[5 + n], halo_recv.at[5 + n], s, down) for n in range(3)]
 
@@ -369,7 +354,32 @@
         def _():
             gz_down[n].start()
 
+
+    def mlp_outer(k, _):
+        mlp_pair(k, 0)
+        return 0
+
+    lax.fori_loop(0, 3, mlp_outer, 0)
+    lax.fori_loop(0, 2, finish, 0)
+    lax.fori_loop(14, 16, finish, 0)
     send_row(0)
+    after = {1: [(stage_a, 0)], 3: [(stage_a, 1)], 5: [(stage_a, 2)]}
+
+    def mlp(k, _):
+        mlp_pair(k // 2, 1 + k % 2)
+        for at, steps in after.items():
+
+            @pl.when(k == at)
+            def _():
+                for step, chunk in steps:
+                    step(chunk)
+
+        return 0
+
+    lax.fori_loop(0, 6, mlp, 0)
+    lax.fori_loop(2, 14, finish, 0)
+    stage_b(0)
+    send_row(1)
 
     lane = lax.broadcasted_iota(jnp.int32, (8, 128), 1)
     sub = lax.broadcasted_iota(jnp.int32, (8, 128), 0)
@@ -400,8 +410,11 @@
 
         @pl.when(g == 5)
         def _():
-            send_row(1)
             stage_b(1)
+            send_row(2)
+
+        @pl.when(g == 8)
+        def _():
             stage_c(0)
 
         return 0
@@ -410,7 +423,6 @@
 
     stage_a(3)
     stage_b(2)
-    send_row(2)
     lax.fori_loop(0, 16, finish_out, 0)
     block_out = pltpu.make_async_copy(outs, out_block.at[0, 0], out_sem.at[0])
     block_out.start()
@@ -560,7 +572,7 @@
         V((768, 192), BF16), V((8, 192, 256), BF16),
         V((8, 192, 256), BF16), V((8, 8, 256), F32), V((8, 192, 256), F32), V((8, 192, 256), F32), V((8, 192, 256), BF16),
         V((8, 192, 256), BF16), V((2, 3, 192, 256), F32), V((16, 8, 128), F32), V((2, 3, 192, 256), BF16),
-        V((3, 16, 48, 128), BF16), V((3, 15, 48, 128), BF16), V((3, 8, 48, 128), F32), V((3, 16, 48, 128), BF16),
+        V((3, 16, 48, 128), BF16), V((3, 15, 48, 128), BF16), V((3, 8, 48, 128), BF16), V((3, 16, 48, 128), BF16),
         V((15, 8, 128), F32), V((8, 8, 128), F32), V((16, 8, 128), F32),
         DMA((2,)), DMA((5,)), DMA((8,)), DMA((8,)), DMA((4, 37)), DMA((4, 37)),
     ]

time: 76.4 us -> 75.4 us (0.987)
  Pallas kernels: 75.6 us -> 74.6 us
    pallas_call x1, Pallas kernels: 72.9 us -> 71.8 us  [on_device(): pl.pallas_call(kernel, out_shape=(jax.ShapeDtypeStruct((1, 1, 8, 192, 256...]
where the time goes in v7:
time: 75.4 us; the launch traced here: 75.2 us
  Pallas kernels  74.6 us (99%)
    pallas_call x1, Pallas kernels, on_device(): pl.pallas_call(kernel, out_shape=(jax.ShapeDtypeStruct((1, 1, 8, 192, 256...  71.8 us
    pallas_call x1, Pallas kernels, hand_over(): pl.pallas_call(hand_over_kernel, out_shape=shapes, in_specs=[pl.BlockSpec...  2.72 us

profile of v7, /device:TPU:1, one launch (start us, length us, event | category | flops | bytes accessed | tf_op | source)
XLA Modules:
  0.0 75.2 jit_solution(1465591384713439378)
XLA Ops:
  0.6 71.8 %shard_map.146 = (bf16[1,1,8,192,256]{4,3,2,1,0:T(8,128)(2,1)}, bf16[1,1,8,192,256]{4,3,2,1,0:T(8,128)(2,1)}, bf16[3,16,48,128]{3,2,1,0:T(8,128)(2,1)}, f32[7,7,192]{2,1,0:T(8,128)}) custom-call(bf16[1,1,8,192,256]{4,3,2,1,0:T(8,128)(2,1)} %bitcast.11, bf16[1,1,8,192,256]{4,3,2,1,0:T(8,128)(2,1)} %bitcast.12, f32[7,7,192]{2,1,0:T(8,128)} %dwk.1, ...), custom_call_target="tpu_custom_call" | custom-call | tf_op jit(solution)/shard_map/pallas_call | solution.py:579
  72.5 2.7 %shard_map.147 = (bf16[1,1,8,192,256]{4,3,2,1,0:T(8,128)(2,1)}, bf16[1,1,8,192,256]{4,3,2,1,0:T(8,128)(2,1)}, f32[7,7,192]{2,1,0:T(8,128)}, f32[192,768]{1,0:T(8,128)}, f32[192,768]{1,0:T(8,128)}) custom-call(bf16[1,1,8,192,256]{4,3,2,1,0:T(8,128)(2,1)} %get-tuple-element.14.block, bf16[1,1,8,192,256]{4,3,2,1,0:T(8,128)(2,1)} %get-tuple-element.15.gin, ...), custom_call_target="tpu_custom_call" | custom-call | tf_op jit(solution)/shard_map/pallas_call | solution.py:552

commit v8 on v5

--- a/solution.py
+++ b/solution.py
@@ -343,23 +343,6 @@
     def full_out(f):
         return pltpu.make_async_copy(full.at[f], out_full.at[f], out_sem.at[2 + f])
 
-    after = {
-        2: [(stage0, 0)], 4: [(stage1, 0)], 5: [(stage0, 1)], 7: [(stage2, 0), (stage1, 1)], 8: [(stage0, 2)],
-    }
-
-    def mlp(k, _):
-        mlp_pair(k // 3, k % 3)
-        for at, steps in after.items():
-
-            @pl.when(k == at)
-            def _():
-                for step, chunk in steps:
-                    step(chunk)
-
-        return 0
-
-    lax.fori_loop(0, 9, mlp, 0)
-
     def finish(n, _):
         i = n // 2
         ln = pl.ds(pl.multiple_of(n % 2 * 128, 128), 128)
@@ -377,8 +360,6 @@
         outs[i, :, ln] = (fx[i + 3, :, ln].astype(F32) + par[4, 0:192, :] * branch).astype(BF16)
         return 0
 
-    lax.fori_loop(0, 16, finish, 0)
-
     gz_up = [remote(gzs.at[n], halo.at[1, n], halo_send.at[2 + n], halo_recv.at[2 + n], s, up) for n in range(3)]
     gz_down = [remote(gzs.at[7 - n], halo.at[0, 2 - n], halo_send.at[5 + n], halo_recv.at[5 + n], s, down) for n in range(3)]
 
@@ -391,10 +372,32 @@
         def _():
             gz_down[n].start()
 
+    def mlp_outer(k, _):
+        mlp_pair(k, 0)
+        return 0
+
+    lax.fori_loop(0, 3, mlp_outer, 0)
+    lax.fori_loop(0, 2, finish, 0)
+    lax.fori_loop(14, 16, finish, 0)
+    send_row(0)
+    after = {1: [(stage0, 0)], 3: [(stage0, 1), (stage1, 0)], 5: [(stage0, 2), (stage1, 1)]}
+
+    def mlp(k, _):
+        mlp_pair(k // 2, 1 + k % 2)
+        for at, steps in after.items():
+
+            @pl.when(k == at)
+            def _():
+                for step, chunk in steps:
+                    step(chunk)
+
+        return 0
+
+    lax.fori_loop(0, 6, mlp, 0)
+    lax.fori_loop(2, 14, finish, 0)
     stage1(2)
-    send_row(0)
-    stage2(1)
-    stage3(0)
+    stage2(0)
+    send_row(1)
 
     lane = lax.broadcasted_iota(jnp.int32, (8, 128), 1)
     sub = lax.broadcasted_iota(jnp.int32, (8, 128), 0)
@@ -423,12 +426,16 @@
     def taps_step(g, _):
         taps_grad(g, 0)
 
-        @pl.when(g == 5)
+        @pl.when(g == 4)
+        def _():
+            stage2(1)
+            stage3(0)
+            send_row(2)
+
+        @pl.when(g == 8)
         def _():
             stage2(2)
-            send_row(1)
             stage3(1)
-            stage4(0)
 
         return 0
 
@@ -439,9 +446,7 @@
     k_core = remote(gkr.at[other], k0, k_send.at[0], k_recv.at[0], partner, t)
     k_core.start()
     stage3(2)
-    send_row(2)
-    stage4(1)
-    stage5(0)
+    stage4(0)
     lax.fori_loop(0, 16, finish_out, 0)
     block_out = pltpu.make_async_copy(outs, out_block.at[0, 0], out_sem.at[0])
     block_out.start()
@@ -460,9 +465,9 @@
     for c in ky_copies:
         c.start()
     build_taps(dwk, flat, back, back_h, True)
+    stage4(1)
+    stage5(0)
     stage4(2)
-    stage5(1)
-    stage6(0)
     lax.fori_loop(0, 4, back_own, 0)
     for c in ky_copies:
         c.wait()
@@ -470,8 +475,9 @@
     kx_copies = [remote(kx.at[x], kx.at[x], k_send.at[4 + d], k_recv.at[4 + d], *x_peers[d]) for d in range(3)]
     for c in kx_copies:
         c.start()
+    stage5(1)
     stage5(2)
-    stage6(1)
+    stage6(0)
     lax.fori_loop(4, 12, back_own, 0)
     for c in kx_copies:
         c.wait()
@@ -479,6 +485,7 @@
     kz_copies = [remote(kz.at[z], kz.at[z], k_send.at[7 + d], k_recv.at[7 + d], *z_peers[d]) for d in range(3)]
     for c in kz_copies:
         c.start()
+    stage6(1)
     stage6(2)
     stage7(0)
     stage7(1)

time: 74.6 us -> 71.2 us (0.954); the launches traced: 73.6 us -> 70.9 us
  Pallas kernels: 72.9 us -> 70.3 us
    pallas_call x1, Pallas kernels: 70.2 us -> 67.6 us  [on_device(): pl.pallas_call(kernel, out_shape=(jax.ShapeDtypeStruct((1, 1, 8, 192, 256...]
where the time goes in v8:
time: 71.2 us; the launch traced here: 70.9 us
  Pallas kernels  70.3 us (99%)
    pallas_call x1, Pallas kernels, on_device(): pl.pallas_call(kernel, out_shape=(jax.ShapeDtypeStruct((1, 1, 8, 192, 256...  67.6 us
    pallas_call x1, Pallas kernels, hand_over(): pl.pallas_call(hand_over_kernel, out_shape=shapes, in_specs=[pl.BlockSpec...  2.72 us

profile of v8, /device:TPU:1, one launch (start us, length us, event | category | flops | bytes accessed | tf_op | source)
XLA Modules:
  0.0 70.9 jit_solution(11984632300860276969)
XLA Ops:
  0.6 67.6 %shard_map.146 = (bf16[1,1,8,192,256]{4,3,2,1,0:T(8,128)(2,1)}, bf16[1,1,8,192,256]{4,3,2,1,0:T(8,128)(2,1)}, bf16[3,2,192,256]{3,2,1,0:T(8,128)(2,1)}, f32[7,7,192]{2,1,0:T(8,128)}) custom-call(bf16[1,1,8,192,256]{4,3,2,1,0:T(8,128)(2,1)} %bitcast.11, bf16[1,1,8,192,256]{4,3,2,1,0:T(8,128)(2,1)} %bitcast.12, f32[7,7,192]{2,1,0:T(8,128)} %dwk.1, ...), custom_call_target="tpu_custom_call" | custom-call | tf_op jit(solution)/shard_map/pallas_call | solution.py:619
  68.2 2.7 %shard_map.147 = (bf16[1,1,8,192,256]{4,3,2,1,0:T(8,128)(2,1)}, bf16[1,1,8,192,256]{4,3,2,1,0:T(8,128)(2,1)}, f32[7,7,192]{2,1,0:T(8,128)}, f32[192,768]{1,0:T(8,128)}, f32[192,768]{1,0:T(8,128)}) custom-call(bf16[1,1,8,192,256]{4,3,2,1,0:T(8,128)(2,1)} %get-tuple-element.14.block, bf16[1,1,8,192,256]{4,3,2,1,0:T(8,128)(2,1)} %get-tuple-element.15.gin, ...), custom_call_target="tpu_custom_call" | custom-call | tf_op jit(solution)/shard_map/pallas_call | solution.py:591

commit v9 on v8

--- a/solution.py
+++ b/solution.py
@@ -394,10 +394,12 @@
         return 0
 
     lax.fori_loop(0, 6, mlp, 0)
-    lax.fori_loop(2, 14, finish, 0)
+    lax.fori_loop(2, 4, finish, 0)
+    lax.fori_loop(12, 14, finish, 0)
     stage1(2)
     stage2(0)
     send_row(1)
+    lax.fori_loop(4, 12, finish, 0)
 
     lane = lax.broadcasted_iota(jnp.int32, (8, 128), 1)
     sub = lax.broadcasted_iota(jnp.int32, (8, 128), 0)

time: 71.2 us -> 71.1 us (level)
  no operation moved by 1% of the time
where the time goes in v9:
time: 71.1 us; the launch traced here: 70.9 us
  Pallas kernels  70.3 us (99%)
    pallas_call x1, Pallas kernels, on_device(): pl.pallas_call(kernel, out_shape=(jax.ShapeDtypeStruct((1, 1, 8, 192, 256...  67.6 us
    pallas_call x1, Pallas kernels, hand_over(): pl.pallas_call(hand_over_kernel, out_shape=shapes, in_specs=[pl.BlockSpec...  2.72 us

profile of v9, /device:TPU:1, one launch (start us, length us, event | category | flops | bytes accessed | tf_op | source)
XLA Modules:
  0.0 70.9 jit_solution(4460384513715524277)
XLA Ops:
  0.6 67.6 %shard_map.146 = (bf16[1,1,8,192,256]{4,3,2,1,0:T(8,128)(2,1)}, bf16[1,1,8,192,256]{4,3,2,1,0:T(8,128)(2,1)}, bf16[3,2,192,256]{3,2,1,0:T(8,128)(2,1)}, f32[7,7,192]{2,1,0:T(8,128)}) custom-call(bf16[1,1,8,192,256]{4,3,2,1,0:T(8,128)(2,1)} %bitcast.11, bf16[1,1,8,192,256]{4,3,2,1,0:T(8,128)(2,1)} %bitcast.12, f32[7,7,192]{2,1,0:T(8,128)} %dwk.1, ...), custom_call_target="tpu_custom_call" | custom-call | tf_op jit(solution)/shard_map/pallas_call | solution.py:621
  68.2 2.7 %shard_map.147 = (bf16[1,1,8,192,256]{4,3,2,1,0:T(8,128)(2,1)}, bf16[1,1,8,192,256]{4,3,2,1,0:T(8,128)(2,1)}, f32[7,7,192]{2,1,0:T(8,128)}, f32[192,768]{1,0:T(8,128)}, f32[192,768]{1,0:T(8,128)}) custom-call(bf16[1,1,8,192,256]{4,3,2,1,0:T(8,128)(2,1)} %get-tuple-element.14.block, bf16[1,1,8,192,256]{4,3,2,1,0:T(8,128)(2,1)} %get-tuple-element.15.gin, ...), custom_call_target="tpu_custom_call" | custom-call | tf_op jit(solution)/shard_map/pallas_call | solution.py:593
